TPU v7x, 128 devices: a whole 4x4x4 slice. The times are simulated.
128 devices in a mesh: pool: 32 (over y, x, core), grp: 4 (over z).
Axes of the slice: x: 4, y: 4, z: 4, core: 2. Of those that a mesh axis runs over, the one named last changes fastest.
Arguments:
- mel_rows: bfloat16 [4096, 1920], P(('grp', 'pool')), parts along dimension 0, may hold values from -6 to 6
- old_cache: bfloat16 [8192, 6656], P(('grp', 'pool')), parts along dimension 0, may hold values from -6 to 6
- new_owner: int32 [4096, 1], P('grp'), parts along dimension 0, may hold values from 0 to 31; in each aligned block of 32 rows (0 to 31, 32 to 63, ...) at most 2 rows name the same one
- prev_owner: int32 [4096, 1], P('grp'), parts along dimension 0, may hold values from 0 to 31; in each aligned block of 32 rows (0 to 31, 32 to 63, ...) at most 2 rows name the same one
- active: int32 [4096], P('grp'), parts along dimension 0, may hold values 0 or 1
- w_pre: bfloat16 [560, 512], replicated, may hold values from -0.25 to 0.25
- w_up: bfloat16 [1024, 2048], replicated, may hold values from -0.1875 to 0.1875
- res_first: bfloat16 [3, 768, 256], replicated, may hold values from -0.21875 to 0.21875
- res_second: bfloat16 [3, 768, 256], replicated, may hold values from -0.21875 to 0.21875
Outputs:
- wave_features: bfloat16 [4096, 36864], P(('grp', 'pool')), parts along dimension 0
- new_cache: bfloat16 [8192, 6656], P(('grp', 'pool')), parts along dimension 0
There are 4 independent parts, one for each index of `grp`. A program takes and returns all parts, laid end to end along the dimension named above; an argument that names none is the same for every part. Nothing has to cross between parts.
Inputs may be any that keep to these rules, and one draw needn't show every extreme that they name: `new_owner`: among the 32 utterances of one home no owner is named more than 2 times, a bound that some block reaches. `prev_owner`: among the 32 utterances of one home no owner is named more than 2 times, a bound that some block reaches.
All inputs are finite; a program needn't handle non-finite values.
Results may differ from a plain program's by a relative error of at most 0.0058.
Values may be sent and summed in bfloat16 or wider, within the bound.
A program may use at most 128 MiB of HBM per device.

v0:
```python
import jax
import jax.numpy as jnp
from jax import lax
from jax.sharding import PartitionSpec as P

C0 = 512
C1 = 256
MELS = 80
UP = 8
FRAMES = 18
LOOK = 6


DILATIONS = (1, 3, 5)
SLOPE = 0.1


def leaky_relu(values):
    return jnp.where(values >= 0, values, SLOPE * values)


def shifted_columns(sequence, dilation, length):
    return jnp.concatenate(
        [
            sequence[:, tap_index * dilation : tap_index * dilation + length, :]
            for tap_index in range(3)
        ],
        axis=-1,
    )


def vocode(mel_block, caches, w_pre, w_up, res_first, res_second):
    rows_here = mel_block.shape[0]
    frames_in = mel_block.reshape(rows_here, FRAMES + LOOK, MELS)
    window = jnp.concatenate(
        [frames_in[:, tap_index : tap_index + FRAMES, :] for tap_index in range(LOOK + 1)], axis=-1
    )
    window = window.reshape(rows_here * FRAMES, (LOOK + 1) * MELS)
    pre_out = jnp.dot(window, w_pre, preferred_element_type=jnp.float32).reshape(
        rows_here, FRAMES, C0
    )
    pre_last = caches[:, :C0].reshape(rows_here, 1, C0)
    up_input = jnp.concatenate([pre_last, leaky_relu(pre_out).astype(jnp.bfloat16)], axis=1)
    paired = jnp.concatenate([up_input[:, :-1], up_input[:, 1:]], axis=-1).reshape(
        rows_here * FRAMES, 2 * C0
    )
    length = UP * FRAMES
    stream = jnp.dot(paired, w_up, preferred_element_type=jnp.float32).reshape(
        rows_here, length, C1
    )
    kept_parts = [up_input[:, FRAMES]]
    offset = C0
    for section, dilation in enumerate(DILATIONS):
        first_hist = caches[:, offset : offset + 2 * dilation * C1].reshape(
            rows_here, 2 * dilation, C1
        )
        offset = offset + 2 * dilation * C1
        second_hist = caches[:, offset : offset + 2 * C1].reshape(rows_here, 2, C1)
        offset = offset + 2 * C1
        first_seq = jnp.concatenate([first_hist, leaky_relu(stream).astype(jnp.bfloat16)], axis=1)
        inner_out = jnp.dot(
            shifted_columns(first_seq, dilation, length).reshape(rows_here * length, 3 * C1),
            res_first[section],
            preferred_element_type=jnp.float32,
        )
        second_seq = jnp.concatenate(
            [
                second_hist,
                leaky_relu(inner_out).astype(jnp.bfloat16).reshape(rows_here, length, C1),
            ],
            axis=1,
        )
        outer_out = jnp.dot(
            shifted_columns(second_seq, 1, length).reshape(rows_here * length, 3 * C1),
            res_second[section],
            preferred_element_type=jnp.float32,
        )
        stream = stream + outer_out.reshape(rows_here, length, C1)
        kept_parts.append(first_seq[:, length:].reshape(rows_here, 2 * dilation * C1))
        kept_parts.append(second_seq[:, length:].reshape(rows_here, 2 * C1))
    wave_out = stream.astype(jnp.bfloat16).reshape(rows_here, length * C1)
    fresh_cache = jnp.concatenate(kept_parts, axis=1)
    return (wave_out, fresh_cache)


def ranks_of(owners):
    members = owners.shape[1]
    same_owner = owners[:, :, None] == owners[:, None, :]
    earlier = jnp.arange(members)[None, :] < jnp.arange(members)[:, None]
    return jnp.sum((same_owner & earlier[None]).astype(jnp.int32), axis=2)


def on_device(
    mel_rows, old_cache, new_owner, prev_owner, active, w_pre, w_up, res_first, res_second
):
    pool_size = lax.axis_size("pool")
    position = lax.axis_index("pool")
    rows_here = mel_rows.shape[0]
    slot_total = old_cache.shape[0]
    capacity = slot_total // pool_size
    cache_width = old_cache.shape[1]
    my_new = lax.dynamic_slice_in_dim(new_owner[:, 0], position * rows_here, rows_here)
    my_prev = lax.dynamic_slice_in_dim(prev_owner[:, 0], position * rows_here, rows_here)
    my_active = lax.dynamic_slice_in_dim(active, position * rows_here, rows_here)
    my_new_rank = ranks_of(my_new[None])[0]
    my_prev_rank = ranks_of(my_prev[None])[0]
    arrived = lax.all_to_all(
        old_cache.reshape(pool_size, capacity, cache_width),
        "pool",
        split_axis=0,
        concat_axis=0,
        tiled=True,
    )
    arrived = arrived.reshape(slot_total, cache_width)
    picking = (
        (my_prev * capacity + my_prev_rank)[:, None] == jnp.arange(slot_total)[None, :]
    ).astype(jnp.bfloat16)
    held_cache = jnp.dot(picking, arrived, preferred_element_type=jnp.float32).astype(
        jnp.bfloat16
    )
    wave_out, fresh_cache = vocode(mel_rows, held_cache, w_pre, w_up, res_first, res_second)
    live_rows = (my_active == 1)[:, None]
    wave_features = jnp.where(live_rows, wave_out, jnp.zeros_like(wave_out))
    kept_cache = jnp.where(live_rows, fresh_cache, held_cache)
    slot_ids = my_new * capacity + my_new_rank
    placing = (jnp.arange(slot_total)[:, None] == slot_ids[None, :]).astype(jnp.bfloat16)
    sent_cache = jnp.dot(placing, kept_cache, preferred_element_type=jnp.float32).astype(
        jnp.bfloat16
    )
    new_cache = lax.all_to_all(
        sent_cache.reshape(pool_size, capacity, cache_width),
        "pool",
        split_axis=0,
        concat_axis=0,
        tiled=True,
    ).reshape(slot_total, cache_width)
    return (wave_features, new_cache)


def solution(mesh):
    return jax.shard_map(
        on_device,
        mesh=mesh,
        in_specs=(
            P(("grp", "pool"), None),
            P(("grp", "pool"), None),
            P("grp", None),
            P("grp", None),
            P("grp"),
            P(),
            P(),
            P(),
            P(),
        ),
        out_specs=(P(("grp", "pool"), None), P(("grp", "pool"), None)),
        check_vma=False,
    )
```

profile of v0, /device:TPU:1, one launch (start us, length us, event | category | flops | bytes accessed | tf_op | source)
XLA Modules:
  0.0 104.0 jit_solution(12861193678217365047)
XLA Ops:
  0.6 0.0 copy-start
  0.6 3.0 %reshape.309 = bf16[32,2,6656]{2,1,0:T(2,128)(2,1)} reshape(bf16[64,6656]{1,0:T(8,128)(2,1)} %param.10) | data formatting | bytes 1703936 | tf_op jit(solution)/shard_map/reshape | solution.py:108
  3.7 8.6 %all-to-all-start = ((bf16[32,2,6656]{2,1,0:T(2,128)(2,1)}), bf16[32,2,6656]{2,1,0:T(2,128)(2,1)S(1)}, u32[]{:S(2)}, u32[]{:S(2)}) async-start(bf16[32,2,6656]{2,1,0:T(2,128)(2,1)} %reshape.309), calls=%async_computation | async-start | bytes 1703936 | tf_op jit(solution)/shard_map/all_to_all | solution.py:107
  12.3 1.2 %reshape.312 = bf16[32,24,80]{2,1,0:T(8,128)(2,1)S(1)} reshape(bf16[32,1920]{1,0:T(8,128)(2,1)} %param.9) | data formatting | bytes 245760 | tf_op jit(solution)/shard_map/reshape | solution.py:34
  13.4 0.3 fusion.84
  13.9 0.7 fusion.79
  14.6 0.2 convert_reduce_fusion.1
  14.8 0.7 fusion.78
  15.6 0.2 convert_reduce_fusion
  15.8 0.7 concatenate.54
  16.5 0.8 dynamic-slice_compare_fusion
  17.2 0.0 copy-done
  17.2 0.6 fusion.47
  17.9 0.6 fusion.73
  18.5 8.8 %all-to-all-done = bf16[32,2,6656]{2,1,0:T(2,128)(2,1)S(1)} async-done(((bf16[32,2,6656]{2,1,0:T(2,128)(2,1)}), bf16[32,2,6656]{2,1,0:T(2,128)(2,1)S(1)}, u32[]{:S(2)}, u32[]{:S(2)}) %all-to-all-start) | async-done | bytes 852000 | tf_op jit(solution)/shard_map/all_to_all | solution.py:107
  27.3 0.3 reshape.310
  27.7 0.3 convolution_convert_fusion.1
  28.0 0.0 copy-start.2
  28.0 0.1 fusion.48
  28.2 0.7 copy.26
  28.8 0.4 reshape.313
  29.3 6.4 %fusion.85 = f32[576,2048]{1,0:T(8,128)} fusion(bf16[576,1024]{1,0:T(8,128)(2,1)S(1)} %reshape.313, bf16[1024,2048]{1,0:T(8,128)(2,1)} %param.15), kind=kOutput, calls=%fused_computation.118 | convolution fusion | flops 2415919104 | bytes 10092544 | tf_op jit(solution)/shard_map/dot_general | solution.py:48
  35.7 0.0 copy-done.2
  35.7 6.0 %reshape.314 = f32[32,144,256]{2,1,0:T(8,128)} reshape(f32[576,2048]{1,0:T(8,128)} %fusion.85) | data formatting | bytes 9437184 | tf_op jit(solution)/shard_map/reshape | solution.py:48
  41.6 2.9 %fusion.27 = bf16[32,144,256]{2,1,0:T(8,128)(2,1)S(1)} fusion(f32[32,144,256]{2,1,0:T(8,128)} %reshape.314), kind=kLoop, calls=%fused_computation.38 | loop fusion | flops 4718592 | bytes 7077888 | tf_op jit(solution)/shard_map/convert_element_type | solution.py:60
  44.6 1.4 %fusion.37 = bf16[32,144,256]{2,1,0:T(8,128)(2,1)S(1)} fusion(bf16[32,2,256]{2,1,0:T(2,128)(2,1)S(1)} %reshape.316, bf16[32,144,256]{2,1,0:T(8,128)(2,1)S(1)} %fusion.27), kind=kLoop, calls=%fused_computation.62 | loop fusion | flops 4718592 | bytes 4751360 | tf_op jit(solution)/shard_map/concatenate | solution.py:60
  46.0 1.1 %fusion.20 = bf16[32,144,768]{2,1,0:T(8,128)(2,1)S(1)} fusion(bf16[32,144,256]{2,1,0:T(8,128)(2,1)S(1)} %fusion.27, bf16[32,2,256]{2,1,0:T(2,128)(2,1)S(1)} %reshape.316, bf16[32,144,256]{2,1,0:T(8,128)(2,1)S(1)} %fusion.37), kind=kLoop, calls=%fused_computation.31 | loop fusion | flops 28311552 | bytes 11829248 | tf_op jit(solution)/shard_map/concatenate | solution.py:23
  47.2 3.0 %fusion.28 = bf16[4608,256]{1,0:T(8,128)(2,1)S(1)} fusion(bf16[4608,768]{1,0:T(8,128)(2,1)S(1)} %bitcast.78, bf16[3,768,256]{2,1,0:T(8,128)(2,1)} %param.16), kind=kOutput, calls=%fused_computation.39 | convolution fusion | flops 1816657920 | bytes 9830400 | tf_op jit(solution)/shard_map/dot_general | solution.py:61
  50.2 0.0 copy-start.6
  50.3 1.3 %copy-done.6 = bf16[4608,256]{1,0:T(8,128)(2,1)} copy-done((bf16[4608,256]{1,0:T(8,128)(2,1)}, bf16[4608,256]{1,0:T(8,128)(2,1)S(1)}, u32[]{:S(2)}) %copy-start.6) | copy-done | bytes 2359320
  51.6 1.4 %fusion.36 = bf16[32,144,256]{2,1,0:T(8,128)(2,1)S(1)} fusion(bf16[32,2,256]{2,1,0:T(2,128)(2,1)S(1)} %reshape.315, bf16[32,144,256]{2,1,0:T(8,128)(2,1)S(1)} %bitcast.85), kind=kLoop, calls=%fused_computation.61 | loop fusion | flops 4718592 | bytes 4751360 | tf_op jit(solution)/shard_map/concatenate | solution.py:66
  53.0 0.0 slice-start
  53.0 7.2 %fusion.29 = (bf16[32,144,256]{2,1,0:T(8,128)(2,1)S(1)}, f32[32,144,256]{2,1,0:T(8,128)}) fusion(f32[32,144,256]{2,1,0:T(8,128)} %reshape.314, bf16[3,768,256]{2,1,0:T(8,128)(2,1)} %param.17, bf16[32,144,256]{2,1,0:T(8,128)(2,1)} %bitcast.86, bf16[32,2,256]{2,1,0:T(2,128)(2,1)S(1)} %reshape.315, bf16[32,144,256]{2,1,0:T(8,128)(2,1)S(1)} %fusion.36), kind=kOutput, calls=%fused_computation.40 | convolution fusion | flops 1846149120 | bytes 16941056 | tf_op jit(solution)/shard_map/dot_general | solution.py:73
  60.3 0.0 slice-done
  60.3 0.1 reshape.320
  60.4 1.4 %fusion.35 = bf16[32,144,256]{2,1,0:T(8,128)(2,1)S(1)} fusion(bf16[32,6,256]{2,1,0:T(8,128)(2,1)S(1)} %reshape.320, bf16[32,144,256]{2,1,0:T(8,128)(2,1)S(1)} %get-tuple-element.14), kind=kLoop, calls=%fused_computation.60 | loop fusion | flops 4718592 | bytes 4816896 | tf_op jit(solution)/shard_map/concatenate | solution.py:60
  61.9 1.2 %fusion.13 = bf16[32,144,768]{2,1,0:T(8,128)(2,1)S(1)} fusion(bf16[32,144,256]{2,1,0:T(8,128)(2,1)S(1)} %get-tuple-element.14, bf16[32,6,256]{2,1,0:T(8,128)(2,1)S(1)} %reshape.320, bf16[32,144,256]{2,1,0:T(8,128)(2,1)S(1)} %fusion.35), kind=kLoop, calls=%fused_computation.23 | loop fusion | flops 28311552 | bytes 11894784 | tf_op jit(solution)/shard_map/concatenate | solution.py:23
  63.1 3.0 %fusion.30 = bf16[4608,256]{1,0:T(8,128)(2,1)S(1)} fusion(bf16[4608,768]{1,0:T(8,128)(2,1)S(1)} %bitcast.79, bf16[3,768,256]{2,1,0:T(8,128)(2,1)} %param.16), kind=kOutput, calls=%fused_computation.41 | convolution fusion | flops 1816657920 | bytes 9830400 | tf_op jit(solution)/shard_map/dot_general | solution.py:61
  66.1 0.0 copy-start.7
  66.2 1.4 %fusion.34 = bf16[32,144,256]{2,1,0:T(8,128)(2,1)S(1)} fusion(bf16[32,2,256]{2,1,0:T(2,128)(2,1)S(1)} %reshape.319, bf16[32,144,256]{2,1,0:T(8,128)(2,1)S(1)} %bitcast.88), kind=kLoop, calls=%fused_computation.59 | loop fusion | flops 4718592 | bytes 4751360 | tf_op jit(solution)/shard_map/concatenate | solution.py:66
  67.6 0.0 copy-done.7
  67.6 0.0 slice-start.1
  67.6 7.1 %fusion.31 = (bf16[32,144,256]{2,1,0:T(8,128)(2,1)S(1)}, f32[32,144,256]{2,1,0:T(8,128)}) fusion(f32[32,144,256]{2,1,0:T(8,128)} %get-tuple-element.15, bf16[3,768,256]{2,1,0:T(8,128)(2,1)} %param.17, bf16[32,144,256]{2,1,0:T(8,128)(2,1)} %bitcast.89, bf16[32,2,256]{2,1,0:T(2,128)(2,1)S(1)} %reshape.319, bf16[32,144,256]{2,1,0:T(8,128)(2,1)S(1)} %fusion.34), kind=kOutput, calls=%fused_computation.42 | convolution fusion | flops 1846149120 | bytes 16941056 | tf_op jit(solution)/shard_map/dot_general | solution.py:73
  74.7 0.1 slice.191
  74.8 0.1 copy.39
  74.8 0.0 slice-done.1
  74.9 0.1 reshape.324
  75.0 1.3 %fusion.38 = bf16[32,144,256]{2,1,0:T(8,128)(2,1)S(1)} fusion(bf16[32,10,256]{2,1,0:T(8,128)(2,1)S(1)} %reshape.324, bf16[32,144,256]{2,1,0:T(8,128)(2,1)S(1)} %get-tuple-element.16), kind=kLoop, calls=%fused_computation.63 | loop fusion | flops 4718592 | bytes 4882432 | tf_op jit(solution)/shard_map/concatenate | solution.py:60
  76.3 1.2 %fusion.6 = bf16[32,144,768]{2,1,0:T(8,128)(2,1)S(1)} fusion(bf16[32,144,256]{2,1,0:T(8,128)(2,1)S(1)} %get-tuple-element.16, bf16[32,10,256]{2,1,0:T(8,128)(2,1)S(1)} %reshape.324, bf16[32,144,256]{2,1,0:T(8,128)(2,1)S(1)} %fusion.38), kind=kLoop, calls=%fused_computation.15 | loop fusion | flops 28311552 | bytes 11960320 | tf_op jit(solution)/shard_map/concatenate | solution.py:23
  77.5 0.0 copy-start.3
  77.5 3.1 %fusion.32 = bf16[4608,256]{1,0:T(8,128)(2,1)S(1)} fusion(bf16[4608,768]{1,0:T(8,128)(2,1)S(1)} %bitcast.80, bf16[3,768,256]{2,1,0:T(8,128)(2,1)} %param.16), kind=kOutput, calls=%fused_computation.43 | convolution fusion | flops 1816657920 | bytes 9830400 | tf_op jit(solution)/shard_map/dot_general | solution.py:61
  80.6 0.0 copy-start.4
  80.8 1.2 %copy-done.4 = bf16[4608,256]{1,0:T(8,128)(2,1)} copy-done((bf16[4608,256]{1,0:T(8,128)(2,1)}, bf16[4608,256]{1,0:T(8,128)(2,1)S(1)}, u32[]{:S(2)}) %copy-start.4) | copy-done | bytes 2359320
  82.0 0.4 convolution_convert_fusion
  82.4 1.2 %reshape.334 = bf16[32,2,6656]{2,1,0:T(2,128)(2,1)} reshape(bf16[64,6656]{1,0:T(8,128)(2,1)S(1)} %convolution_convert_fusion) | data formatting | bytes 1703936 | tf_op jit(solution)/shard_map/reshape | solution.py:131
  83.7 4.0 %all-to-all-start.1 = ((bf16[32,2,6656]{2,1,0:T(2,128)(2,1)}), bf16[32,2,6656]{2,1,0:T(2,128)(2,1)S(1)}, u32[]{:S(2)}, u32[]{:S(2)}) async-start(bf16[32,2,6656]{2,1,0:T(2,128)(2,1)} %reshape.334), calls=%async_computation.1 | async-start | bytes 1703936 | tf_op jit(solution)/shard_map/all_to_all | solution.py:130
  87.7 0.0 copy-start.5
  87.7 3.3 %fusion.33 = bf16[32,144,256]{2,1,0:T(8,128)(2,1)S(1)} fusion(bf16[32,2,256]{2,1,0:T(2,128)(2,1)S(1)} %reshape.323, bf16[32,144,256]{2,1,0:T(8,128)(2,1)} %bitcast.82), kind=kLoop, calls=%fused_computation.58 | loop fusion | flops 4718592 | bytes 4751360 | tf_op jit(solution)/shard_map/concatenate | solution.py:66
  91.0 4.6 %add_convert_fusion = bf16[32,144,256]{2,1,0:T(8,128)(2,1)S(1)} fusion(f32[32,144,256]{2,1,0:T(8,128)} %get-tuple-element.17, bf16[32,144,256]{2,1,0:T(8,128)(2,1)S(1)} %bitcast.83, bf16[32,2,256]{2,1,0:T(2,128)(2,1)S(1)} %reshape.323, bf16[32,144,256]{2,1,0:T(8,128)(2,1)S(1)} %fusion.33, bf16[3,768,256]{2,1,0:T(8,128)(2,1)} %param.17), kind=kOutput, calls=%fused_computation.44 | convolution fusion | flops 1842610176 | bytes 12222464 | tf_op jit(solution)/shard_map/dot_general | solution.py:73
  95.6 0.0 copy-start.1
  95.6 0.9 copy.34
  96.6 1.6 %broadcast_select_fusion = bf16[32,36864]{1,0:T(8,128)(2,1)} fusion(bf16[32,36864]{1,0:T(8,128)(2,1)S(1)} %bitcast.77, pred[32]{0:T(512)(128)(4,1)S(1)} %dynamic-slice_compare_fusion), kind=kLoop, calls=%fused_computation.64 | loop fusion | flops 1179648 | bytes 4718624 | tf_op jit(solution)/shard_map/jit(_where)/select_n | solution.py:123
  98.2 4.6 %all-to-all-done.1 = bf16[32,2,6656]{2,1,0:T(2,128)(2,1)S(1)} async-done(((bf16[32,2,6656]{2,1,0:T(2,128)(2,1)}), bf16[32,2,6656]{2,1,0:T(2,128)(2,1)S(1)}, u32[]{:S(2)}, u32[]{:S(2)}) %all-to-all-start.1) | async-done | bytes 852000 | tf_op jit(solution)/shard_map/all_to_all | solution.py:130
  102.8 1.2 %reshape.335 = bf16[64,6656]{1,0:T(8,128)(2,1)} reshape(bf16[32,2,6656]{2,1,0:T(2,128)(2,1)S(1)} %all-to-all-done.1) | data formatting | bytes 1703936 | tf_op jit(solution)/shard_map/reshape | solution.py:136
  (34 shorter events, 0.5 us)
Async XLA Ops:
  0.6 16.6 %copy-start = (bf16[560,512]{1,0:T(8,128)(2,1)S(1)}, bf16[560,512]{1,0:T(8,128)(2,1)}, u32[]{:S(2)}) copy-start(bf16[560,512]{1,0:T(8,128)(2,1)} %param.14) | copy-start | bytes 1720324
  3.7 23.7 %all-to-all-start = ((bf16[32,2,6656]{2,1,0:T(2,128)(2,1)}), bf16[32,2,6656]{2,1,0:T(2,128)(2,1)S(1)}, u32[]{:S(2)}, u32[]{:S(2)}) async-start(bf16[32,2,6656]{2,1,0:T(2,128)(2,1)} %reshape.309), calls=%async_computation | async-start | bytes 1703936 | tf_op jit(solution)/shard_map/all_to_all | solution.py:107
  28.0 7.7 %copy-start.2 = (bf16[32,6656]{1,0:T(8,128)(2,1)}, bf16[32,6656]{1,0:T(8,128)(2,1)S(1)}, u32[]{:S(2)}) copy-start(bf16[32,6656]{1,0:T(8,128)(2,1)S(1)} %convolution_convert_fusion.1) | copy-start | bytes 1277956
  50.2 1.4 %copy-start.6 = (bf16[4608,256]{1,0:T(8,128)(2,1)}, bf16[4608,256]{1,0:T(8,128)(2,1)S(1)}, u32[]{:S(2)}) copy-start(bf16[4608,256]{1,0:T(8,128)(2,1)S(1)} %fusion.28) | copy-start | bytes 7077892
  53.0 7.3 %slice-start = ((bf16[32,6656]{1,0:T(8,128)(2,1)}), bf16[32,1536]{1,0:T(8,128)(2,1)S(1)}, s32[]{:S(2)}) async-start(bf16[32,6656]{1,0:T(8,128)(2,1)} %copy-done.2), calls=%async_computation.2 | async-start | bytes 196608 | tf_op jit(solution)/shard_map/slice | solution.py:54
  66.1 1.5 %copy-start.7 = (bf16[4608,256]{1,0:T(8,128)(2,1)}, bf16[4608,256]{1,0:T(8,128)(2,1)S(1)}, u32[]{:S(2)}) copy-start(bf16[4608,256]{1,0:T(8,128)(2,1)S(1)} %fusion.30) | copy-start | bytes 7077892
  67.6 7.2 %slice-start.1 = ((bf16[32,6656]{1,0:T(8,128)(2,1)}), bf16[32,2560]{1,0:T(8,128)(2,1)S(1)}, s32[]{:S(2)}) async-start(bf16[32,6656]{1,0:T(8,128)(2,1)} %copy-done.2), calls=%async_computation.3 | async-start | bytes 327680 | tf_op jit(solution)/shard_map/slice | solution.py:54
  77.5 3.2 %copy-start.8 = (bf16[32,6656]{1,0:T(8,128)(2,1)S(1)}, bf16[32,6656]{1,0:T(8,128)(2,1)}, u32[]{:S(2)}) copy-start(bf16[32,6656]{1,0:T(8,128)(2,1)} %fusion.73) | copy-start | bytes 1277956
  77.5 4.5 %copy-start.3 = (bf16[32,6656]{1,0:T(8,128)(2,1)S(1)}, bf16[32,6656]{1,0:T(8,128)(2,1)}, u32[]{:S(2)}) copy-start(bf16[32,6656]{1,0:T(8,128)(2,1)} %copy-done.2) | copy-start | bytes 1277956
  80.6 1.4 %copy-start.4 = (bf16[4608,256]{1,0:T(8,128)(2,1)}, bf16[4608,256]{1,0:T(8,128)(2,1)S(1)}, u32[]{:S(2)}) copy-start(bf16[4608,256]{1,0:T(8,128)(2,1)S(1)} %fusion.32) | copy-start | bytes 7077892
  83.7 19.1 %all-to-all-start.1 = ((bf16[32,2,6656]{2,1,0:T(2,128)(2,1)}), bf16[32,2,6656]{2,1,0:T(2,128)(2,1)S(1)}, u32[]{:S(2)}, u32[]{:S(2)}) async-start(bf16[32,2,6656]{2,1,0:T(2,128)(2,1)} %reshape.334), calls=%async_computation.1 | async-start | bytes 1703936 | tf_op jit(solution)/shard_map/all_to_all | solution.py:130
  87.7 3.3 %copy-start.5 = (bf16[4608,256]{1,0:T(8,128)(2,1)S(1)}, bf16[4608,256]{1,0:T(8,128)(2,1)}, u32[]{:S(2)}) copy-start(bf16[4608,256]{1,0:T(8,128)(2,1)} %copy-done.4) | copy-start | bytes 7077892
  95.6 8.4 %copy-start.1 = (bf16[560,512]{1,0:T(8,128)(2,1)S(1)}, bf16[560,512]{1,0:T(8,128)(2,1)}, u32[]{:S(2)}) copy-start(bf16[560,512]{1,0:T(8,128)(2,1)} %param.14) | copy-start | bytes 1720324
where the time goes:
time: 105 us; the launch traced here: 104 us
  matrix products  35.8 us (34%)
  local copies, waits for them, and re-layouts  20.7 us (20%)
  other arithmetic  20.4 us (19%)
  waiting for transfers between devices  13.5 us (13%)
  starting transfers between devices  12.6 us (12%)
  between operations  1.17 us (1%)
    dot_general x3, matrix products, vocode(): jnp.dot(shifted_columns(second_seq, 1, length).reshape(rows_here * length...  18.9 us
    dot_general x3, matrix products, vocode(): jnp.dot(shifted_columns(first_seq, dilation, length).reshape(rows_here *...  9.1 us
    all_to_all x1, waiting for transfers between devices, on_device(): lax.all_to_all(old_cache.reshape(pool_size, capacity, cache_width), 'pool...  8.84 us
    all_to_all x1, starting transfers between devices, on_device(): lax.all_to_all(old_cache.reshape(pool_size, capacity, cache_width), 'pool...  8.59 us
    dot_general x1, matrix products, vocode(): jnp.dot(paired, w_up, preferred_element_type=jnp.float32)  6.41 us
    concatenate x3, other arithmetic, vocode(): jnp.concatenate([second_hist, leaky_relu(inner_out).astype(jnp.bfloat16)....  6.15 us
    reshape x1, local copies, waits for them, and re-layouts, vocode(): jnp.dot(paired, w_up, preferred_element_type=jnp.float32)  5.96 us
    all_to_all x1, waiting for transfers between devices, on_device(): lax.all_to_all(sent_cache.reshape(pool_size, capacity, cache_width), 'poo...  4.61 us
  transfers between devices with their start and end apart: 2, of which 2 were waited for; matrix products, arithmetic and copies ran while one was open for 16% of the time, Pallas kernels for 0%

commit v1 on v0

v1 whole, which is shorter than its diff:
```python
import jax
import jax.numpy as jnp
from jax import lax
from jax.experimental import pallas as pl
from jax.experimental.pallas import tpu as pltpu
from jax.sharding import PartitionSpec as P

C0 = 512
C1 = 256
MELS = 80
UP = 8
FRAMES = 18
LOOK = 6


DILATIONS = (1, 3, 5)
SLOPE = 0.1
BLOCK = 16
CHUNK = 384


def leaky_relu(values):
    return jnp.where(values >= 0, values, SLOPE * values)


def vocode_kernel(
    win_ref, held_ref, act_ref, wpre_ref, wup_ref, rf_ref, rs_ref,
    wave_ref, kept_ref, x_ref, a_ref, e_ref,
):
    rows = held_ref.shape[0]
    length = UP * FRAMES
    live = act_ref[...] == 1
    win = win_ref[...].reshape(FRAMES * rows, win_ref.shape[2])
    pre = jnp.dot(win, wpre_ref[...], preferred_element_type=jnp.float32)
    pre_act = leaky_relu(pre).astype(jnp.bfloat16)
    up_input = jnp.concatenate([held_ref[:, :C0], pre_act], axis=0)
    paired = jnp.concatenate([up_input[: FRAMES * rows], up_input[rows:]], axis=1)
    prod = jnp.dot(paired, wup_ref[...], preferred_element_type=jnp.float32)
    for t in range(FRAMES):
        for j in range(UP):
            x_ref[pl.ds((UP * t + j) * rows, rows), :] = prod[
                t * rows : (t + 1) * rows, j * C1 : (j + 1) * C1
            ]
    kept_ref[:, :C0] = jnp.where(live, pre_act[(FRAMES - 1) * rows :], held_ref[:, :C0])
    offset = C0
    steps = length * rows // CHUNK
    for section, dilation in enumerate(DILATIONS):
        for p in range(2 * dilation):
            a_ref[pl.ds(p * rows, rows), :] = held_ref[:, offset + p * C1 : offset + (p + 1) * C1]
        a_off = offset
        offset = offset + 2 * dilation * C1
        for p in range(2):
            e_ref[pl.ds(p * rows, rows), :] = held_ref[:, offset + p * C1 : offset + (p + 1) * C1]
        e_off = offset
        offset = offset + 2 * C1

        def fill(c, carry, dilation=dilation):
            r = pl.multiple_of(c * CHUNK, CHUNK)
            a_ref[pl.ds(2 * dilation * rows + r, CHUNK), :] = leaky_relu(
                x_ref[pl.ds(r, CHUNK), :]
            ).astype(jnp.bfloat16)
            return carry

        lax.fori_loop(0, steps, fill, 0)

        def first(c, carry, dilation=dilation, section=section):
            r = pl.multiple_of(c * CHUNK, CHUNK)
            z = jnp.dot(
                a_ref[pl.ds(r, CHUNK), :], rf_ref[section, 0:C1, :],
                preferred_element_type=jnp.float32,
            )
            for k in (1, 2):
                z = z + jnp.dot(
                    a_ref[pl.ds(pl.multiple_of(r + k * dilation * rows, 16), CHUNK), :],
                    rf_ref[section, k * C1 : (k + 1) * C1, :],
                    preferred_element_type=jnp.float32,
                )
            e_ref[pl.ds(pl.multiple_of(2 * rows + r, 16), CHUNK), :] = leaky_relu(z).astype(
                jnp.bfloat16
            )
            return carry

        lax.fori_loop(0, steps, first, 0)

        def second(c, carry, section=section):
            r = pl.multiple_of(c * CHUNK, CHUNK)
            z = x_ref[pl.ds(r, CHUNK), :]
            for k in range(3):
                z = z + jnp.dot(
                    e_ref[pl.ds(pl.multiple_of(r + k * rows, 16), CHUNK), :],
                    rs_ref[section, k * C1 : (k + 1) * C1, :],
                    preferred_element_type=jnp.float32,
                )
            x_ref[pl.ds(r, CHUNK), :] = z
            return carry

        lax.fori_loop(0, steps, second, 0)
        for p in range(2 * dilation):
            kept_ref[:, a_off + p * C1 : a_off + (p + 1) * C1] = jnp.where(
                live,
                a_ref[pl.ds((length + p) * rows, rows), :],
                held_ref[:, a_off + p * C1 : a_off + (p + 1) * C1],
            )
        for p in range(2):
            kept_ref[:, e_off + p * C1 : e_off + (p + 1) * C1] = jnp.where(
                live,
                e_ref[pl.ds((length + p) * rows, rows), :],
                held_ref[:, e_off + p * C1 : e_off + (p + 1) * C1],
            )
    for n in range(length):
        wave_ref[:, n * C1 : (n + 1) * C1] = jnp.where(
            live, x_ref[pl.ds(n * rows, rows), :], 0.0
        ).astype(jnp.bfloat16)


def vocode(mel_block, caches, live, w_pre, w_up, res_first, res_second):
    rows_here = mel_block.shape[0]
    cache_width = caches.shape[1]
    length = UP * FRAMES
    span = (LOOK + 1) * MELS
    window = jnp.stack(
        [mel_block[:, t * MELS : t * MELS + span] for t in range(FRAMES)], axis=0
    )
    block = BLOCK
    const2 = lambda i: (0, 0)
    const3 = lambda i: (0, 0, 0)
    flops = 2 * rows_here * (FRAMES * span * C0 + FRAMES * 2 * C0 * UP * C1 + 6 * length * 3 * C1 * C1)
    wave, kept = pl.pallas_call(
        vocode_kernel,
        grid=(rows_here // block,),
        in_specs=[
            pl.BlockSpec((FRAMES, block, span), lambda i: (0, i, 0)),
            pl.BlockSpec((block, cache_width), lambda i: (i, 0)),
            pl.BlockSpec((block, 1), lambda i: (i, 0)),
            pl.BlockSpec(w_pre.shape, const2),
            pl.BlockSpec(w_up.shape, const2),
            pl.BlockSpec(res_first.shape, const3),
            pl.BlockSpec(res_second.shape, const3),
        ],
        out_specs=[
            pl.BlockSpec((block, length * C1), lambda i: (i, 0)),
            pl.BlockSpec((block, cache_width), lambda i: (i, 0)),
        ],
        out_shape=[
            jax.ShapeDtypeStruct((rows_here, length * C1), jnp.bfloat16),
            jax.ShapeDtypeStruct((rows_here, cache_width), jnp.bfloat16),
        ],
        scratch_shapes=[
            pltpu.VMEM((length * block, C1), jnp.float32),
            pltpu.VMEM(((length + 10) * block, C1), jnp.bfloat16),
            pltpu.VMEM(((length + 2) * block, C1), jnp.bfloat16),
        ],
        compiler_params=pltpu.CompilerParams(vmem_limit_bytes=60 * 1024 * 1024),
        cost_estimate=pl.CostEstimate(flops=flops, transcendentals=0, bytes_accessed=12 * 1024 * 1024),
    )(window, caches, live, w_pre, w_up, res_first, res_second)
    return wave, kept


def ranks_of(owners):
    members = owners.shape[1]
    same_owner = owners[:, :, None] == owners[:, None, :]
    earlier = jnp.arange(members)[None, :] < jnp.arange(members)[:, None]
    return jnp.sum((same_owner & earlier[None]).astype(jnp.int32), axis=2)


def on_device(
    mel_rows, old_cache, new_owner, prev_owner, active, w_pre, w_up, res_first, res_second
):
    pool_size = lax.axis_size("pool")
    position = lax.axis_index("pool")
    rows_here = mel_rows.shape[0]
    slot_total = old_cache.shape[0]
    capacity = slot_total // pool_size
    cache_width = old_cache.shape[1]
    my_new = lax.dynamic_slice_in_dim(new_owner[:, 0], position * rows_here, rows_here)
    my_prev = lax.dynamic_slice_in_dim(prev_owner[:, 0], position * rows_here, rows_here)
    my_active = lax.dynamic_slice_in_dim(active, position * rows_here, rows_here)
    my_new_rank = ranks_of(my_new[None])[0]
    my_prev_rank = ranks_of(my_prev[None])[0]
    arrived = lax.all_to_all(
        old_cache.reshape(pool_size, capacity, cache_width),
        "pool",
        split_axis=0,
        concat_axis=0,
        tiled=True,
    )
    arrived = arrived.reshape(slot_total, cache_width)
    picking = (
        (my_prev * capacity + my_prev_rank)[:, None] == jnp.arange(slot_total)[None, :]
    ).astype(jnp.bfloat16)
    held_cache = jnp.dot(picking, arrived, preferred_element_type=jnp.float32).astype(
        jnp.bfloat16
    )
    wave_features, kept_cache = vocode(
        mel_rows, held_cache, my_active[:, None], w_pre, w_up, res_first, res_second
    )
    slot_ids = my_new * capacity + my_new_rank
    placing = (jnp.arange(slot_total)[:, None] == slot_ids[None, :]).astype(jnp.bfloat16)
    sent_cache = jnp.dot(placing, kept_cache, preferred_element_type=jnp.float32).astype(
        jnp.bfloat16
    )
    new_cache = lax.all_to_all(
        sent_cache.reshape(pool_size, capacity, cache_width),
        "pool",
        split_axis=0,
        concat_axis=0,
        tiled=True,
    ).reshape(slot_total, cache_width)
    return (wave_features, new_cache)


def solution(mesh):
    return jax.shard_map(
        on_device,
        mesh=mesh,
        in_specs=(
            P(("grp", "pool"), None),
            P(("grp", "pool"), None),
            P("grp", None),
            P("grp", None),
            P("grp"),
            P(),
            P(),
            P(),
            P(),
        ),
        out_specs=(P(("grp", "pool"), None), P(("grp", "pool"), None)),
        check_vma=False,
    )
```

time: 105 us -> 83.7 us (0.80)
  matrix products: 35.8 us -> 2.44 us
  Pallas kernels: 0 us -> 33.1 us
  other arithmetic: 20.4 us -> 1.1 us
  blocking collectives: 0 us -> 18.6 us
  local copies, waits for them, and re-layouts: 20.7 us -> 7.72 us
  starting transfers between devices: 12.6 us -> 8.59 us
  waiting for transfers between devices: 13.5 us -> 11 us
    dot_general x8 -> x0, matrix products: 35 us -> none  [the longest x3 18.9 us: vocode(): jnp.dot(shifted_columns(second_seq, 1, length).reshape(rows_here * length...]
    pallas_call x0 -> x1, Pallas kernels: none -> 33.1 us  [vocode(): pl.pallas_call(vocode_kernel, grid=(rows_here // block,), in_specs=[pl.Bl...]
    all_to_all x0 -> x1, blocking collectives: none -> 18.6 us  [on_device(): lax.all_to_all(sent_cache.reshape(pool_size, capacity, cache_width), 'poo...]
    concatenate x10 -> x0, other arithmetic: 13.9 us -> none  [the longest x3 6.15 us: vocode(): jnp.concatenate([second_hist, leaky_relu(inner_out).astype(jnp.bfloat16)....]
    reshape x9 -> x0, local copies, waits for them, and re-layouts: 7.81 us -> none  [the longest x1 5.96 us: vocode(): jnp.dot(paired, w_up, preferred_element_type=jnp.float32)]
    all_to_all x1 -> x0, waiting for transfers between devices: 4.61 us -> none  [on_device(): lax.all_to_all(sent_cache.reshape(pool_size, capacity, cache_width), 'poo...]
    all_to_all x1 -> x0, starting transfers between devices: 3.97 us -> none  [on_device(): lax.all_to_all(sent_cache.reshape(pool_size, capacity, cache_width), 'poo...]
    unnamed x38 -> x23, local copies, waits for them, and re-layouts: 4.44 us -> 1.27 us
  transfers between devices with their start and end apart: 2 -> 1, of which waited for: 2 -> 1; matrix products, arithmetic and copies ran while one was open for 16% -> 5% of each run, Pallas kernels for 0% -> 0%
where the time goes in v1:
time: 83.7 us; the launch traced here: 83.4 us
  Pallas kernels  33.1 us (40%)
  blocking collectives  18.6 us (22%)
  waiting for transfers between devices  11 us (13%)
  starting transfers between devices  8.59 us (10%)
  local copies, waits for them, and re-layouts  7.72 us (9%)
  matrix products  2.44 us (3%)
  other arithmetic  1.1 us (1%)
    pallas_call x1, Pallas kernels, vocode(): pl.pallas_call(vocode_kernel, grid=(rows_here // block,), in_specs=[pl.Bl...  33.1 us
    all_to_all x1, blocking collectives, on_device(): lax.all_to_all(sent_cache.reshape(pool_size, capacity, cache_width), 'poo...  18.6 us
    all_to_all x1, waiting for transfers between devices, on_device(): lax.all_to_all(old_cache.reshape(pool_size, capacity, cache_width), 'pool...  11 us
    all_to_all x1, starting transfers between devices, on_device(): lax.all_to_all(old_cache.reshape(pool_size, capacity, cache_width), 'pool...  8.59 us
    reshape x1, local copies, waits for them, and re-layouts, on_device(): old_cache.reshape(pool_size, capacity, cache_width)  3 us
  transfers between devices with their start and end apart: 1, of which 1 were waited for; matrix products, arithmetic and copies ran while one was open for 5% of the time, Pallas kernels for 0%

profile of v1, /device:TPU:1, one launch (start us, length us, event | category | flops | bytes accessed | tf_op | source)
XLA Modules:
  0.0 83.4 jit_solution(8909416188697850469)
XLA Ops:
  0.6 0.0 copy-start
  0.6 0.0 copy-start.1
  0.7 3.0 %reshape.196 = bf16[32,2,6656]{2,1,0:T(2,128)(2,1)} reshape(bf16[64,6656]{1,0:T(8,128)(2,1)} %param.10) | data formatting | bytes 1703936 | tf_op jit(solution)/shard_map/reshape | solution.py:181
  3.7 8.6 %all-to-all-start = ((bf16[32,2,6656]{2,1,0:T(2,128)(2,1)}), bf16[32,2,6656]{2,1,0:T(2,128)(2,1)S(1)}, u32[]{:S(2)}, u32[]{:S(2)}) async-start(bf16[32,2,6656]{2,1,0:T(2,128)(2,1)} %reshape.196), calls=%async_computation | async-start | bytes 1703936 | tf_op jit(solution)/shard_map/all_to_all | solution.py:180
  12.3 0.0 copy-done
  12.3 0.1 dynamic-slice_bitcast_fusion.1
  12.3 0.7 dynamic-slice_bitcast_fusion
  13.1 0.2 convert_reduce_fusion.1
  13.3 0.2 convert_reduce_fusion
  13.5 0.7 copy.12.act_ref
  14.1 0.0 copy-done.1
  14.2 0.1 bitcast_dynamic-update-slice_fusion.16
  14.2 0.1 bitcast_dynamic-update-slice_fusion.15
  14.3 0.1 bitcast_dynamic-update-slice_fusion.14
  14.4 0.1 bitcast_dynamic-update-slice_fusion.13
  14.5 0.1 bitcast_dynamic-update-slice_fusion.12
  14.6 0.1 bitcast_dynamic-update-slice_fusion.11
  14.7 0.1 bitcast_dynamic-update-slice_fusion.10
  14.8 0.1 bitcast_dynamic-update-slice_fusion.8
  14.9 0.1 bitcast_dynamic-update-slice_fusion.7
  15.0 0.1 bitcast_dynamic-update-slice_fusion.6
  15.1 0.1 bitcast_dynamic-update-slice_fusion.5
  15.2 0.1 bitcast_dynamic-update-slice_fusion.4
  15.2 0.1 bitcast_dynamic-update-slice_fusion.3
  15.3 0.7 fusion.4
  16.1 0.1 bitcast_dynamic-update-slice_fusion.2
  16.2 0.1 bitcast_dynamic-update-slice_fusion.win_ref
  16.3 0.0 copy-start.2
  16.3 11.0 %all-to-all-done = bf16[32,2,6656]{2,1,0:T(2,128)(2,1)S(1)} async-done(((bf16[32,2,6656]{2,1,0:T(2,128)(2,1)}), bf16[32,2,6656]{2,1,0:T(2,128)(2,1)S(1)}, u32[]{:S(2)}, u32[]{:S(2)}) %all-to-all-start) | async-done | bytes 852000 | tf_op jit(solution)/shard_map/all_to_all | solution.py:180
  27.3 0.3 reshape.197
  27.6 1.1 %convolution_convert_fusion.1.held_ref = bf16[32,6656]{1,0:T(8,128)(2,1)} fusion(bf16[64,6656]{1,0:T(8,128)(2,1)S(1)} %reshape.197, s32[32]{0:T(128)S(1)} %fusion.4), kind=kOutput, calls=%fused_computation.1 | convolution fusion | flops 27478016 | bytes 1278080 | tf_op jit(solution)/shard_map/dot_general | solution.py:191
  28.7 0.0 copy-done.2
  28.7 33.1 %shard_map.104 = (bf16[32,36864]{1,0:T(8,128)(2,1)}, bf16[32,6656]{1,0:T(8,128)(2,1)}) custom-call(bf16[18,32,560]{2,1,0:T(8,128)(2,1)} %copy-done.2, bf16[32,6656]{1,0:T(8,128)(2,1)} %convolution_convert_fusion.1.held_ref, s32[32,1]{1,0:T(8,128)} %copy.12.act_ref, bf16[560,512]{1,0:T(8,128)(2,1)} %wpre_ref.1, bf16[1024,2048]{1,0:T(8,128)(2,1)} %wup_ref.1, ...), custom_call_target="tpu_custom_call" | custom-call | flops 13617856512 | bytes 12582912 | tf_op jit(solution)/shard_map/pallas_call | solution.py:128
  61.9 1.4 %convolution_convert_fusion = bf16[64,6656]{1,0:T(8,128)(2,1)S(1)} fusion(bf16[32,6656]{1,0:T(8,128)(2,1)} %get-tuple-element.5, s32[32]{0:T(128)S(1)} %multiply_add_fusion), kind=kOutput, calls=%fused_computation | convolution fusion | flops 27691008 | bytes 1278080 | tf_op jit(solution)/shard_map/dot_general | solution.py:199
  63.2 0.3 reshape.198
  63.6 18.6 %all_to_all.10 = bf16[32,2,6656]{2,1,0:T(2,128)(2,1)S(1)} all-to-all(bf16[32,2,6656]{2,1,0:T(2,128)(2,1)S(1)} %reshape.198), channel_id=1, replica_groups=mesh['pool'=32,'grp'=4] {'pool'}, dimensions={0} | all-to-all | bytes 1703936 | tf_op jit(solution)/shard_map/all_to_all | solution.py:202
  82.1 1.2 %reshape.199 = bf16[64,6656]{1,0:T(8,128)(2,1)} reshape(bf16[32,2,6656]{2,1,0:T(2,128)(2,1)S(1)} %all_to_all.10) | data formatting | bytes 1703936 | tf_op jit(solution)/shard_map/reshape | solution.py:208
  (4 shorter events, 0.0 us)
Async XLA Ops:
  0.6 11.6 %copy-start = (s32[1024]{0:T(1024)S(1)}, s32[1024]{0:T(1024)}, u32[]{:S(2)}) copy-start(s32[1024]{0:T(1024)} %param.13) | copy-start | bytes 12292
  0.6 13.5 %copy-start.1 = (bf16[32,1920]{1,0:T(8,128)(2,1)S(1)}, bf16[32,1920]{1,0:T(8,128)(2,1)}, u32[]{:S(2)}) copy-start(bf16[32,1920]{1,0:T(8,128)(2,1)} %param.9) | copy-start | bytes 368644
  3.7 23.7 %all-to-all-start = ((bf16[32,2,6656]{2,1,0:T(2,128)(2,1)}), bf16[32,2,6656]{2,1,0:T(2,128)(2,1)S(1)}, u32[]{:S(2)}, u32[]{:S(2)}) async-start(bf16[32,2,6656]{2,1,0:T(2,128)(2,1)} %reshape.196), calls=%async_computation | async-start | bytes 1703936 | tf_op jit(solution)/shard_map/all_to_all | solution.py:180
  16.3 12.5 %copy-start.2 = (bf16[18,32,560]{2,1,0:T(8,128)(2,1)}, bf16[18,32,560]{2,1,0:T(8,128)(2,1)S(1)}, u32[]{:S(2)}) copy-start(bf16[18,32,560]{2,1,0:T(8,128)(2,1)S(1)} %bitcast_dynamic-update-slice_fusion.win_ref) | copy-start | bytes 1935364

commit v2 on v1

--- a/solution.py
+++ b/solution.py
@@ -156,6 +156,62 @@
     return wave, kept
 
 
+def exchange_kernel(src_ref, dst_ref, send_sem, recv_sem, local_sem):
+    n = send_sem.shape[0]
+    cap = src_ref.shape[0] // n
+    me = lax.axis_index("pool")
+    barrier = pltpu.get_barrier_semaphore()
+    for s in range(1, n):
+        pl.semaphore_signal(barrier, 1, device_id={"pool": lax.rem(me + s, n)}, device_id_type=pl.DeviceIdType.MESH)
+    pl.semaphore_wait(barrier, n - 1)
+    local = pltpu.make_async_copy(
+        src_ref.at[pl.ds(me * cap, cap)], dst_ref.at[pl.ds(me * cap, cap)], local_sem
+    )
+    local.start()
+    copies = []
+    for s in range(1, n):
+        peer = lax.rem(me + s, n)
+        copy = pltpu.make_async_remote_copy(
+            src_ref=src_ref.at[pl.ds(peer * cap, cap)],
+            dst_ref=dst_ref.at[pl.ds(me * cap, cap)],
+            send_sem=send_sem.at[s],
+            recv_sem=recv_sem.at[s],
+            device_id={"pool": peer},
+            device_id_type=pl.DeviceIdType.MESH,
+        )
+        copy.start()
+        copies.append(copy)
+    for copy in copies:
+        copy.wait_send()
+    for s in range(1, n):
+        source = lax.rem(me + n - s, n)
+        pltpu.make_async_remote_copy(
+            src_ref=src_ref.at[pl.ds(source * cap, cap)],
+            dst_ref=dst_ref.at[pl.ds(source * cap, cap)],
+            send_sem=send_sem.at[s],
+            recv_sem=recv_sem.at[s],
+            device_id={"pool": source},
+            device_id_type=pl.DeviceIdType.MESH,
+        ).wait_recv()
+    local.wait()
+
+
+def exchange(blocks, tag):
+    n = lax.axis_size("pool")
+    return pl.pallas_call(
+        exchange_kernel,
+        in_specs=[pl.BlockSpec(memory_space=pl.ANY)],
+        out_specs=pl.BlockSpec(memory_space=pl.ANY),
+        out_shape=jax.ShapeDtypeStruct(blocks.shape, blocks.dtype),
+        scratch_shapes=[
+            pltpu.SemaphoreType.DMA((n,)),
+            pltpu.SemaphoreType.DMA((n,)),
+            pltpu.SemaphoreType.DMA,
+        ],
+        compiler_params=pltpu.CompilerParams(collective_id=tag, has_side_effects=True),
+    )(blocks)
+
+
 def ranks_of(owners):
     members = owners.shape[1]
     same_owner = owners[:, :, None] == owners[:, None, :]
@@ -177,14 +233,7 @@
     my_active = lax.dynamic_slice_in_dim(active, position * rows_here, rows_here)
     my_new_rank = ranks_of(my_new[None])[0]
     my_prev_rank = ranks_of(my_prev[None])[0]
-    arrived = lax.all_to_all(
-        old_cache.reshape(pool_size, capacity, cache_width),
-        "pool",
-        split_axis=0,
-        concat_axis=0,
-        tiled=True,
-    )
-    arrived = arrived.reshape(slot_total, cache_width)
+    arrived = exchange(old_cache, 0)
     picking = (
         (my_prev * capacity + my_prev_rank)[:, None] == jnp.arange(slot_total)[None, :]
     ).astype(jnp.bfloat16)
@@ -199,13 +248,7 @@
     sent_cache = jnp.dot(placing, kept_cache, preferred_element_type=jnp.float32).astype(
         jnp.bfloat16
     )
-    new_cache = lax.all_to_all(
-        sent_cache.reshape(pool_size, capacity, cache_width),
-        "pool",
-        split_axis=0,
-        concat_axis=0,
-        tiled=True,
-    ).reshape(slot_total, cache_width)
+    new_cache = exchange(sent_cache, 1)
     return (wave_features, new_cache)
 
 

time: 83.7 us -> 96.9 us (1.16)
  Pallas kernels: 33.1 us -> 69.4 us
  blocking collectives: 18.6 us -> 0 us
  local copies, waits for them, and re-layouts: 7.72 us -> 19.9 us
  waiting for transfers between devices: 11 us -> 0 us
  starting transfers between devices: 8.59 us -> 0 us
  matrix products: 2.44 us -> 4.51 us
    pallas_call x0 -> x2, Pallas kernels: none -> 36.3 us  [exchange(): pl.pallas_call(exchange_kernel, in_specs=[pl.BlockSpec(memory_space=pl.AN...]
    all_to_all x1 -> x0, blocking collectives: 18.6 us -> none  [on_device(): lax.all_to_all(sent_cache.reshape(pool_size, capacity, cache_width), 'poo...]
    unnamed x23 -> x22, local copies, waits for them, and re-layouts: 1.27 us -> 17.6 us
    all_to_all x1 -> x0, waiting for transfers between devices: 11 us -> none  [on_device(): lax.all_to_all(old_cache.reshape(pool_size, capacity, cache_width), 'pool...]
    all_to_all x1 -> x0, starting transfers between devices: 8.59 us -> none  [on_device(): lax.all_to_all(old_cache.reshape(pool_size, capacity, cache_width), 'pool...]
    reshape x4 -> x0, local copies, waits for them, and re-layouts: 4.86 us -> none  [the longest x1 3 us: on_device(): old_cache.reshape(pool_size, capacity, cache_width)]
    dot_general x1, matrix products: 1.09 us -> 2.24 us  [on_device(): jnp.dot(picking, arrived, preferred_element_type=jnp.float32)]
  transfers between devices with their start and end apart: 1 -> 0, of which waited for: 1 -> 0; matrix products, arithmetic and copies ran while one was open for 5% -> 0% of each run, Pallas kernels for 0% -> 0%
where the time goes in v2:
time: 96.9 us; the launch traced here: 95.6 us
  Pallas kernels  69.4 us (72%)
  local copies, waits for them, and re-layouts  19.9 us (21%)
  matrix products  4.51 us (5%)
  other arithmetic  1.12 us (1%)
    pallas_call x2, Pallas kernels, exchange(): pl.pallas_call(exchange_kernel, in_specs=[pl.BlockSpec(memory_space=pl.AN...  36.3 us
    pallas_call x1, Pallas kernels, vocode(): pl.pallas_call(vocode_kernel, grid=(rows_here // block,), in_specs=[pl.Bl...  33.1 us
    unnamed x22, local copies, waits for them, and re-layouts  17.6 us
    dot_general x1, matrix products, on_device(): jnp.dot(placing, kept_cache, preferred_element_type=jnp.float32)  2.26 us
    dot_general x1, matrix products, on_device(): jnp.dot(picking, arrived, preferred_element_type=jnp.float32)  2.24 us

profile of v2, /device:TPU:1, one launch (start us, length us, event | category | flops | bytes accessed | tf_op | source)
XLA Modules:
  0.0 95.6 jit_solution(5411122279348073495)
XLA Ops:
  0.6 0.0 copy-start
  0.6 0.7 copy-done
  1.3 0.1 dynamic-slice_bitcast_fusion.1
  1.4 0.7 fusion.5
  2.1 0.2 convert_reduce_fusion.1
  2.3 0.7 fusion.4
  3.1 0.2 convert_reduce_fusion
  3.2 0.7 copy.12.act_ref
  3.9 0.8 bitcast_dynamic-update-slice_fusion.17
  4.7 0.9 bitcast_dynamic-update-slice_fusion.16
  5.6 0.9 bitcast_dynamic-update-slice_fusion.15
  6.5 0.9 bitcast_dynamic-update-slice_fusion.14
  7.4 0.9 bitcast_dynamic-update-slice_fusion.13
  8.3 0.9 bitcast_dynamic-update-slice_fusion.12
  9.2 0.9 bitcast_dynamic-update-slice_fusion.11
  10.0 0.9 bitcast_dynamic-update-slice_fusion.10
  10.9 0.8 bitcast_dynamic-update-slice_fusion.9
  11.7 0.9 bitcast_dynamic-update-slice_fusion.8
  12.6 0.9 bitcast_dynamic-update-slice_fusion.7
  13.5 0.9 bitcast_dynamic-update-slice_fusion.6
  14.4 0.9 bitcast_dynamic-update-slice_fusion.5
  15.3 0.9 bitcast_dynamic-update-slice_fusion.4
  16.2 0.9 bitcast_dynamic-update-slice_fusion.3
  17.0 0.9 bitcast_dynamic-update-slice_fusion.2
  17.9 0.8 bitcast_dynamic-update-slice_fusion.1
  18.7 0.9 bitcast_dynamic-update-slice_fusion.win_ref
  19.6 0.0 copy-start.1
  19.6 20.0 %shard_map.104 = bf16[64,6656]{1,0:T(8,128)(2,1)} custom-call(bf16[64,6656]{1,0:T(8,128)(2,1)} %src_ref.1), custom_call_target="tpu_custom_call" | custom-call | tf_op jit(solution)/shard_map/pallas_call | solution.py:201
  39.6 2.2 %convolution_convert_fusion.1.held_ref = bf16[32,6656]{1,0:T(8,128)(2,1)} fusion(bf16[64,6656]{1,0:T(8,128)(2,1)} %shard_map.104, s32[32]{0:T(128)S(1)} %get-tuple-element.6), kind=kOutput, calls=%fused_computation.1 | convolution fusion | flops 27478016 | bytes 1278080 | tf_op jit(solution)/shard_map/dot_general | solution.py:240
  41.9 0.0 copy-done.1
  41.9 33.1 %shard_map.105 = (bf16[32,36864]{1,0:T(8,128)(2,1)}, bf16[32,6656]{1,0:T(8,128)(2,1)}) custom-call(bf16[18,32,560]{2,1,0:T(8,128)(2,1)} %copy-done.1, bf16[32,6656]{1,0:T(8,128)(2,1)} %convolution_convert_fusion.1.held_ref, s32[32,1]{1,0:T(8,128)} %copy.12.act_ref, bf16[560,512]{1,0:T(8,128)(2,1)} %wpre_ref.1, bf16[1024,2048]{1,0:T(8,128)(2,1)} %wup_ref.1, ...), custom_call_target="tpu_custom_call" | custom-call | flops 13617856512 | bytes 12582912 | tf_op jit(solution)/shard_map/pallas_call | solution.py:128
  75.0 2.3 %convolution_convert_fusion.src_ref = bf16[64,6656]{1,0:T(8,128)(2,1)} fusion(bf16[32,6656]{1,0:T(8,128)(2,1)} %get-tuple-element.5, s32[32]{0:T(128)S(1)} %multiply_add_fusion), kind=kOutput, calls=%fused_computation | convolution fusion | flops 27691008 | bytes 1278080 | tf_op jit(solution)/shard_map/dot_general | solution.py:248
  77.2 16.3 %shard_map.106 = bf16[64,6656]{1,0:T(8,128)(2,1)} custom-call(bf16[64,6656]{1,0:T(8,128)(2,1)} %convolution_convert_fusion.src_ref), custom_call_target="tpu_custom_call" | custom-call | tf_op jit(solution)/shard_map/pallas_call | solution.py:201
  93.5 2.1 %copy.31 = bf16[64,6656]{1,0:T(8,128)(2,1)} copy(bf16[64,6656]{1,0:T(8,128)(2,1)} %shard_map.106) | data formatting | bytes 1703936
  (1 shorter events, 0.0 us)
Async XLA Ops:
  0.6 0.7 copy-start
  19.6 22.3 %copy-start.1 = (bf16[18,32,560]{2,1,0:T(8,128)(2,1)}, bf16[18,32,560]{2,1,0:T(8,128)(2,1)S(1)}, u32[]{:S(2)}) copy-start(bf16[18,32,560]{2,1,0:T(8,128)(2,1)S(1)} %bitcast_dynamic-update-slice_fusion.win_ref) | copy-start | bytes 1935364

commit v3 on v1

v3 whole, which is shorter than its diff:
```python
import jax
import jax.numpy as jnp
from jax import lax
from jax.experimental import pallas as pl
from jax.experimental.pallas import tpu as pltpu
from jax.sharding import PartitionSpec as P

C0 = 512
C1 = 256
MELS = 80
UP = 8
FRAMES = 18
LOOK = 6


DILATIONS = (1, 3, 5)
SLOPE = 0.1
CHUNK = 768


def leaky_relu(values):
    return jnp.where(values >= 0, values, SLOPE * values)


MESH = pl.DeviceIdType.MESH
IN_PIECES = ((0, 1536), (1536, 3584), (3584, 6656))
OUT_PIECES = ((0, 1536), (1536, 3584), (3584, 6144), (6144, 6656))


def fused_kernel(
    mel_ref, old_ref, pick_ref, place_ref, act_ref, wpre_ref, wup_ref, rf_ref, rs_ref,
    wave_ref, new_ref,
    arrived, sendbuf, held, kept, x_ref, a_ref, e_ref,
    in_send, in_recv, in_local, out_send, out_recv, out_local,
):
    n = in_send.shape[1]
    cap = old_ref.shape[0] // n
    rows = held.shape[0]
    length = UP * FRAMES
    me = lax.axis_index("pool")

    barrier = pltpu.get_barrier_semaphore()

    def greet(s, carry):
        pl.semaphore_signal(barrier, 1, device_id={"pool": lax.rem(me + s, n)}, device_id_type=MESH)
        return carry

    lax.fori_loop(1, n, greet, 0)
    pl.semaphore_wait(barrier, n - 1)

    def start_piece(src, dst, lo, hi, sends, recvs, locals_, p):
        cols = pl.ds(lo, hi - lo)
        mine = pl.ds(pl.multiple_of(me * cap, cap), cap)
        pltpu.make_async_copy(src.at[mine, cols], dst.at[mine, cols], locals_.at[p]).start()

        def body(s, carry):
            peer = lax.rem(me + s, n)
            pltpu.make_async_remote_copy(
                src_ref=src.at[pl.ds(pl.multiple_of(peer * cap, cap), cap), cols],
                dst_ref=dst.at[mine, cols],
                send_sem=sends.at[p, s],
                recv_sem=recvs.at[p, s],
                device_id={"pool": peer},
                device_id_type=MESH,
            ).start()
            return carry

        lax.fori_loop(1, n, body, 0)

    def wait_piece(src, dst, lo, hi, sends, recvs, locals_, p):
        cols = pl.ds(lo, hi - lo)
        mine = pl.ds(pl.multiple_of(me * cap, cap), cap)

        def body(s, carry):
            peer = lax.rem(me + s, n)
            source = lax.rem(me + n - s, n)
            pltpu.make_async_remote_copy(
                src_ref=src.at[pl.ds(pl.multiple_of(peer * cap, cap), cap), cols],
                dst_ref=dst.at[mine, cols],
                send_sem=sends.at[p, s],
                recv_sem=recvs.at[p, s],
                device_id={"pool": peer},
                device_id_type=MESH,
            ).wait_send()
            pltpu.make_async_remote_copy(
                src_ref=src.at[pl.ds(pl.multiple_of(source * cap, cap), cap), cols],
                dst_ref=dst.at[pl.ds(pl.multiple_of(source * cap, cap), cap), cols],
                send_sem=sends.at[p, s],
                recv_sem=recvs.at[p, s],
                device_id={"pool": source},
                device_id_type=MESH,
            ).wait_recv()
            return carry

        lax.fori_loop(1, n, body, 0)
        pltpu.make_async_copy(src.at[mine, cols], dst.at[mine, cols], locals_.at[p]).wait()

    def fetch(p):
        wait_piece(old_ref, arrived, *IN_PIECES[p], in_send, in_recv, in_local, p)
        lo, hi = IN_PIECES[p]
        held[:, lo:hi] = jnp.dot(
            pick_ref[...], arrived[:, lo:hi], preferred_element_type=jnp.float32
        ).astype(jnp.bfloat16)

    def post(p):
        lo, hi = OUT_PIECES[p]
        sendbuf[:, lo:hi] = jnp.dot(
            place_ref[...], kept[:, lo:hi], preferred_element_type=jnp.float32
        ).astype(jnp.bfloat16)
        start_piece(sendbuf, new_ref, lo, hi, out_send, out_recv, out_local, p)

    start_piece(old_ref, arrived, *IN_PIECES[0], in_send, in_recv, in_local, 0)
    start_piece(old_ref, arrived, *IN_PIECES[1], in_send, in_recv, in_local, 1)

    live = act_ref[...] == 1
    span = MELS
    pre = jnp.dot(mel_ref[0 : FRAMES * rows, :], wpre_ref[0:span, :], preferred_element_type=jnp.float32)
    for k in range(1, LOOK + 1):
        pre = pre + jnp.dot(
            mel_ref[k * rows : (k + FRAMES) * rows, :],
            wpre_ref[k * span : (k + 1) * span, :],
            preferred_element_type=jnp.float32,
        )
    pre_act = leaky_relu(pre).astype(jnp.bfloat16)
    for j in range(UP):
        cols = slice(j * C1, (j + 1) * C1)
        part = jnp.dot(pre_act, wup_ref[C0 : 2 * C0, cols], preferred_element_type=jnp.float32)
        rest = jnp.dot(
            pre_act[: (FRAMES - 1) * rows], wup_ref[0:C0, cols], preferred_element_type=jnp.float32
        )
        x_ref[pl.ds(j * rows, rows), :] = part[0:rows]
        for t in range(1, FRAMES):
            x_ref[pl.ds((UP * t + j) * rows, rows), :] = (
                part[t * rows : (t + 1) * rows] + rest[(t - 1) * rows : t * rows]
            )

    fetch(0)
    start_piece(old_ref, arrived, *IN_PIECES[2], in_send, in_recv, in_local, 2)
    head = jnp.dot(held[:, 0:C0], wup_ref[0:C0, :], preferred_element_type=jnp.float32)
    for j in range(UP):
        x_ref[pl.ds(j * rows, rows), :] = x_ref[pl.ds(j * rows, rows), :] + head[:, j * C1 : (j + 1) * C1]
    kept[:, 0:C0] = jnp.where(live, pre_act[(FRAMES - 1) * rows :], held[:, 0:C0])

    offset = C0
    steps = length * rows // CHUNK
    for section, dilation in enumerate(DILATIONS):
        if section > 0:
            fetch(section)
        a_off = offset
        for p in range(2 * dilation):
            a_ref[pl.ds(p * rows, rows), :] = held[:, offset + p * C1 : offset + (p + 1) * C1]
        offset = offset + 2 * dilation * C1
        e_off = offset
        for p in range(2):
            e_ref[pl.ds(p * rows, rows), :] = held[:, offset + p * C1 : offset + (p + 1) * C1]
        offset = offset + 2 * C1

        def fill(c, carry, dilation=dilation):
            r = pl.multiple_of(c * CHUNK, CHUNK)
            a_ref[pl.ds(pl.multiple_of(2 * dilation * rows + r, 16), CHUNK), :] = leaky_relu(
                x_ref[pl.ds(r, CHUNK), :]
            ).astype(jnp.bfloat16)
            return carry

        lax.fori_loop(0, steps, fill, 0)
        for p in range(2 * dilation):
            kept[:, a_off + p * C1 : a_off + (p + 1) * C1] = jnp.where(
                live,
                a_ref[pl.ds((length + p) * rows, rows), :],
                held[:, a_off + p * C1 : a_off + (p + 1) * C1],
            )
        if section == 2:
            post(2)

        def first(c, carry, dilation=dilation, section=section):
            r = pl.multiple_of(c * CHUNK, CHUNK)
            z = jnp.dot(
                a_ref[pl.ds(r, CHUNK), :], rf_ref[section, 0:C1, :],
                preferred_element_type=jnp.float32,
            )
            for k in (1, 2):
                z = z + jnp.dot(
                    a_ref[pl.ds(pl.multiple_of(r + k * dilation * rows, 16), CHUNK), :],
                    rf_ref[section, k * C1 : (k + 1) * C1, :],
                    preferred_element_type=jnp.float32,
                )
            e_ref[pl.ds(pl.multiple_of(2 * rows + r, 16), CHUNK), :] = leaky_relu(z).astype(
                jnp.bfloat16
            )
            return carry

        lax.fori_loop(0, steps, first, 0)
        for p in range(2):
            kept[:, e_off + p * C1 : e_off + (p + 1) * C1] = jnp.where(
                live,
                e_ref[pl.ds((length + p) * rows, rows), :],
                held[:, e_off + p * C1 : e_off + (p + 1) * C1],
            )
        post(section if section < 2 else 3)

        def second(c, carry, section=section):
            r = pl.multiple_of(c * CHUNK, CHUNK)
            z = x_ref[pl.ds(r, CHUNK), :]
            for k in range(3):
                z = z + jnp.dot(
                    e_ref[pl.ds(pl.multiple_of(r + k * rows, 16), CHUNK), :],
                    rs_ref[section, k * C1 : (k + 1) * C1, :],
                    preferred_element_type=jnp.float32,
                )
            x_ref[pl.ds(r, CHUNK), :] = z
            return carry

        lax.fori_loop(0, steps, second, 0)
    for m in range(length):
        wave_ref[:, m * C1 : (m + 1) * C1] = jnp.where(
            live, x_ref[pl.ds(m * rows, rows), :], 0.0
        ).astype(jnp.bfloat16)
    for p in range(len(OUT_PIECES)):
        wait_piece(sendbuf, new_ref, *OUT_PIECES[p], out_send, out_recv, out_local, p)


def vocode_exchange(mel_rows, old_cache, picking, placing, live, w_pre, w_up, res_first, res_second):
    n = lax.axis_size("pool")
    rows = mel_rows.shape[0]
    slot_total, width = old_cache.shape
    length = UP * FRAMES
    mel_t = mel_rows.reshape(rows, FRAMES + LOOK, MELS).transpose(1, 0, 2).reshape(-1, MELS)
    vmem = pl.BlockSpec(memory_space=pltpu.VMEM)
    anywhere = pl.BlockSpec(memory_space=pl.ANY)
    flops = 2 * rows * (FRAMES * (LOOK + 1) * MELS * C0 + FRAMES * 2 * C0 * UP * C1 + 6 * length * 3 * C1 * C1)
    return pl.pallas_call(
        fused_kernel,
        in_specs=[vmem, anywhere] + [vmem] * 7,
        out_specs=[vmem, anywhere],
        out_shape=[
            jax.ShapeDtypeStruct((rows, length * C1), jnp.bfloat16),
            jax.ShapeDtypeStruct((slot_total, width), jnp.bfloat16),
        ],
        scratch_shapes=[
            pltpu.VMEM((slot_total, width), jnp.bfloat16),
            pltpu.VMEM((slot_total, width), jnp.bfloat16),
            pltpu.VMEM((rows, width), jnp.bfloat16),
            pltpu.VMEM((rows, width), jnp.bfloat16),
            pltpu.VMEM((length * rows, C1), jnp.float32),
            pltpu.VMEM(((length + 10) * rows, C1), jnp.bfloat16),
            pltpu.VMEM(((length + 2) * rows, C1), jnp.bfloat16),
            pltpu.SemaphoreType.DMA((len(IN_PIECES), n)),
            pltpu.SemaphoreType.DMA((len(IN_PIECES), n)),
            pltpu.SemaphoreType.DMA((len(IN_PIECES),)),
            pltpu.SemaphoreType.DMA((len(OUT_PIECES), n)),
            pltpu.SemaphoreType.DMA((len(OUT_PIECES), n)),
            pltpu.SemaphoreType.DMA((len(OUT_PIECES),)),
        ],
        compiler_params=pltpu.CompilerParams(
            collective_id=0, has_side_effects=True, vmem_limit_bytes=60 * 1024 * 1024
        ),
        cost_estimate=pl.CostEstimate(flops=flops, transcendentals=0, bytes_accessed=16 * 1024 * 1024),
    )(mel_t, old_cache, picking, placing, live, w_pre, w_up, res_first, res_second)


def ranks_of(owners):
    members = owners.shape[1]
    same_owner = owners[:, :, None] == owners[:, None, :]
    earlier = jnp.arange(members)[None, :] < jnp.arange(members)[:, None]
    return jnp.sum((same_owner & earlier[None]).astype(jnp.int32), axis=2)


def on_device(
    mel_rows, old_cache, new_owner, prev_owner, active, w_pre, w_up, res_first, res_second
):
    pool_size = lax.axis_size("pool")
    position = lax.axis_index("pool")
    rows_here = mel_rows.shape[0]
    slot_total = old_cache.shape[0]
    capacity = slot_total // pool_size
    my_new = lax.dynamic_slice_in_dim(new_owner[:, 0], position * rows_here, rows_here)
    my_prev = lax.dynamic_slice_in_dim(prev_owner[:, 0], position * rows_here, rows_here)
    my_active = lax.dynamic_slice_in_dim(active, position * rows_here, rows_here)
    my_new_rank = ranks_of(my_new[None])[0]
    my_prev_rank = ranks_of(my_prev[None])[0]
    picking = (
        (my_prev * capacity + my_prev_rank)[:, None] == jnp.arange(slot_total)[None, :]
    ).astype(jnp.bfloat16)
    slot_ids = my_new * capacity + my_new_rank
    placing = (jnp.arange(slot_total)[:, None] == slot_ids[None, :]).astype(jnp.bfloat16)
    return vocode_exchange(
        mel_rows, old_cache, picking, placing, my_active[:, None], w_pre, w_up, res_first, res_second
    )


def solution(mesh):
    return jax.shard_map(
        on_device,
        mesh=mesh,
        in_specs=(
            P(("grp", "pool"), None),
            P(("grp", "pool"), None),
            P("grp", None),
            P("grp", None),
            P("grp"),
            P(),
            P(),
            P(),
            P(),
        ),
        out_specs=(P(("grp", "pool"), None), P(("grp", "pool"), None)),
        check_vma=False,
    )
```

time: 83.7 us -> 58.7 us (0.70)
  blocking collectives: 18.6 us -> 0 us
  Pallas kernels: 33.1 us -> 47.2 us
  waiting for transfers between devices: 11 us -> 0 us
  starting transfers between devices: 8.59 us -> 0 us
  matrix products: 2.44 us -> 0 us
  other arithmetic: 1.1 us -> 2.38 us
    all_to_all x1 -> x0, blocking collectives: 18.6 us -> none  [on_device(): lax.all_to_all(sent_cache.reshape(pool_size, capacity, cache_width), 'poo...]
    pallas_call x1, Pallas kernels: 33.1 us -> 47.2 us  [vocode_exchange(): pl.pallas_call(fused_kernel, in_specs=[vmem, anywhere] + [vmem] * 7, out_...]
    all_to_all x1 -> x0, waiting for transfers between devices: 11 us -> none  [on_device(): lax.all_to_all(old_cache.reshape(pool_size, capacity, cache_width), 'pool...]
    all_to_all x1 -> x0, starting transfers between devices: 8.59 us -> none  [on_device(): lax.all_to_all(old_cache.reshape(pool_size, capacity, cache_width), 'pool...]
    unnamed x23 -> x6, local copies, waits for them, and re-layouts: 1.27 us -> 4.88 us
    reshape x4 -> x2, local copies, waits for them, and re-layouts: 4.86 us -> 1.86 us  [vocode_exchange(): mel_rows.reshape(rows, FRAMES + LOOK, MELS).transpose(1, 0, 2)]
    dot_general x2 -> x0, matrix products: 2.44 us -> none  [the longest x1 1.36 us: on_device(): jnp.dot(placing, kept_cache, preferred_element_type=jnp.float32)]
    convert_element_type x0 -> x2, other arithmetic: none -> 1.27 us  [the longest x1 0.66 us: on_device(): picking = ((my_prev * capacity + my_prev_rank)[:, None] == jnp.arange(slo...]
  transfers between devices with their start and end apart: 1 -> 0, of which waited for: 1 -> 0; matrix products, arithmetic and copies ran while one was open for 5% -> 0% of each run, Pallas kernels for 0% -> 0%
where the time goes in v3:
time: 58.7 us; the launch traced here: 58.5 us
  Pallas kernels  47.2 us (80%)
  local copies, waits for them, and re-layouts  8.22 us (14%)
  other arithmetic  2.38 us (4%)
  between operations  0.67 us (1%)
    pallas_call x1, Pallas kernels, vocode_exchange(): pl.pallas_call(fused_kernel, in_specs=[vmem, anywhere] + [vmem] * 7, out_...  47.2 us
    unnamed x6, local copies, waits for them, and re-layouts  4.88 us
    reshape x2, local copies, waits for them, and re-layouts, vocode_exchange(): mel_rows.reshape(rows, FRAMES + LOOK, MELS).transpose(1, 0, 2)  1.86 us

profile of v3, /device:TPU:1, one launch (start us, length us, event | category | flops | bytes accessed | tf_op | source)
XLA Modules:
  0.0 58.5 jit_solution(7697806845289099813)
XLA Ops:
  0.6 0.0 copy-start
  0.6 0.7 %copy-done = s32[1024]{0:T(1024)S(1)} copy-done((s32[1024]{0:T(1024)S(1)}, s32[1024]{0:T(1024)}, u32[]{:S(2)}) %copy-start) | copy-done | bytes 4120
  1.3 0.1 dynamic-slice_bitcast_fusion
  1.4 0.7 %fusion.5 = s32[32]{0:T(128)S(1)} fusion(s32[1024,1]{0,1:T(1,128)} %param.12, s32[]{:T(128)S(6)} %select_n.2), kind=kLoop, calls=%fused_computation.15 | loop fusion | bytes 260 | tf_op jit(solution)/shard_map/eq | solution.py:263
  2.1 0.2 convert_reduce_fusion.1
  2.3 0.7 %fusion.4 = (s32[32]{0:T(128)S(1)}, s32[32]{0:T(128)S(1)}) fusion(s32[32]{0:T(128)S(1)} %convert_reduce_fusion.1, s32[1024,1]{0,1:T(1,128)} %param.12, s32[]{:T(128)S(6)} %select_n.2, s32[1024,1]{0,1:T(1,128)} %param.11), kind=kLoop, calls=%fused_computation.10 | loop fusion | flops 64 | bytes 644 | tf_op jit(solution)/shard_map/eq | solution.py:282
  3.1 0.2 convert_reduce_fusion
  3.2 0.7 %fusion.3.pick_ref = bf16[32,64]{1,0:T(8,128)(2,1)} fusion(s32[32]{0:T(128)S(1)} %get-tuple-element.2), kind=kLoop, calls=%fused_computation.8 | loop fusion | flops 4096 | bytes 4224 | tf_op jit(solution)/shard_map/convert_element_type | solution.py:283
  3.9 0.6 %fusion.place_ref = bf16[64,32]{1,0:T(8,128)(2,1)} fusion(s32[32]{0:T(128)S(1)} %multiply_add_fusion), kind=kLoop, calls=%fused_computation.1 | loop fusion | flops 4096 | bytes 4224 | tf_op jit(solution)/shard_map/convert_element_type | solution.py:285
  4.5 0.7 %copy.14.act_ref = s32[32,1]{1,0:T(8,128)} copy(s32[32,1]{0,1:T(1,128)S(1)} %dynamic-slice_bitcast_fusion) | data formatting | bytes 256 | tf_op jit(solution)/shard_map/broadcast_in_dim | solution.py:287
  5.2 1.2 %reshape.190 = bf16[32,24,80]{2,1,0:T(8,128)(2,1)S(1)} reshape(bf16[32,1920]{1,0:T(8,128)(2,1)} %param.9) | data formatting | bytes 245760 | tf_op jit(solution)/shard_map/reshape | solution.py:227
  6.4 0.7 %copy.13 = bf16[32,24,80]{2,0,1:T(8,128)(2,1)} copy(bf16[32,24,80]{2,1,0:T(8,128)(2,1)S(1)} %reshape.190) | data formatting | bytes 245760 | tf_op jit(solution)/shard_map/reshape | solution.py:227
  7.1 47.2 %shard_map.104 = (bf16[32,36864]{1,0:T(8,128)(2,1)}, bf16[64,6656]{1,0:T(8,128)(2,1)}) custom-call(bf16[768,80]{1,0:T(8,128)(2,1)} %bitcast.15, bf16[64,6656]{1,0:T(8,128)(2,1)} %old_ref.1, bf16[32,64]{1,0:T(8,128)(2,1)} %fusion.3.pick_ref, bf16[64,32]{1,0:T(8,128)(2,1)} %fusion.place_ref, s32[32,1]{1,0:T(8,128)} %copy.14.act_ref, ...), custom_call_target="tpu_custom_call" | custom-call | flops 13617856512 | bytes 16777216 | tf_op jit(solution)/shard_map/pallas_call | solution.py:231
  54.3 0.0 copy-start.1
  54.3 3.3 %copy.17 = bf16[32,36864]{1,0:T(8,128)(2,1)} copy(bf16[32,36864]{1,0:T(8,128)(2,1)} %get-tuple-element.6) | data formatting | bytes 4718592
  57.6 0.0 copy-done.1
  57.6 0.9 %copy.18 = bf16[64,6656]{1,0:T(8,128)(2,1)} copy(bf16[64,6656]{1,0:T(8,128)(2,1)S(1)} %copy-done.1) | data formatting | bytes 1703936
  (1 shorter events, 0.0 us)
Async XLA Ops:
  0.6 0.7 %copy-start = (s32[1024]{0:T(1024)S(1)}, s32[1024]{0:T(1024)}, u32[]{:S(2)}) copy-start(s32[1024]{0:T(1024)} %param.13) | copy-start | bytes 12292
  54.3 3.3 %copy-start.1 = (bf16[64,6656]{1,0:T(8,128)(2,1)S(1)}, bf16[64,6656]{1,0:T(8,128)(2,1)}, u32[]{:S(2)}) copy-start(bf16[64,6656]{1,0:T(8,128)(2,1)} %get-tuple-element.7) | copy-start | bytes 2555908

commit v4 on v3

--- a/solution.py
+++ b/solution.py
@@ -27,10 +27,29 @@
 OUT_PIECES = ((0, 1536), (1536, 3584), (3584, 6144), (6144, 6656))
 
 
+def slot_tables(new_col, prev_col, rows, slots, cap):
+    ids = lax.broadcasted_iota(jnp.int32, (rows, rows), 0)
+    other = lax.broadcasted_iota(jnp.int32, (rows, rows), 1)
+    diagonal = ids == other
+    new_row = jnp.sum(jnp.where(diagonal, new_col, 0), axis=0, keepdims=True)
+    prev_row = jnp.sum(jnp.where(diagonal, prev_col, 0), axis=0, keepdims=True)
+    prev_rank = jnp.sum(
+        jnp.where((prev_col == prev_row) & (other < ids), 1, 0), axis=1, keepdims=True
+    )
+    new_rank = jnp.sum(jnp.where((new_col == new_row) & (ids < other), 1, 0), axis=0, keepdims=True)
+    picking = (
+        lax.broadcasted_iota(jnp.int32, (rows, slots), 1) == prev_col * cap + prev_rank
+    ).astype(jnp.bfloat16)
+    placing = (
+        lax.broadcasted_iota(jnp.int32, (slots, rows), 0) == new_row * cap + new_rank
+    ).astype(jnp.bfloat16)
+    return picking, placing
+
+
 def fused_kernel(
-    mel_ref, old_ref, pick_ref, place_ref, act_ref, wpre_ref, wup_ref, rf_ref, rs_ref,
+    mel_ref, old_ref, new_owner_ref, prev_owner_ref, act_ref, wpre_ref, wup_ref, rf_ref, rs_ref,
     wave_ref, new_ref,
-    arrived, sendbuf, held, kept, x_ref, a_ref, e_ref,
+    arrived, sendbuf, held, kept, x_ref, a_ref, e_ref, mel_t, pick_ref, place_ref,
     in_send, in_recv, in_local, out_send, out_recv, out_local,
 ):
     n = in_send.shape[1]
@@ -38,6 +57,7 @@
     rows = held.shape[0]
     length = UP * FRAMES
     me = lax.axis_index("pool")
+    mine_rows = pl.ds(pl.multiple_of(me * rows, rows), rows)
 
     barrier = pltpu.get_barrier_semaphore()
 
@@ -112,12 +132,23 @@
     start_piece(old_ref, arrived, *IN_PIECES[0], in_send, in_recv, in_local, 0)
     start_piece(old_ref, arrived, *IN_PIECES[1], in_send, in_recv, in_local, 1)
 
-    live = act_ref[...] == 1
+    picking, placing = slot_tables(
+        new_owner_ref[mine_rows, :], prev_owner_ref[mine_rows, :], rows, old_ref.shape[0], cap
+    )
+    pick_ref[...] = picking
+    place_ref[...] = placing
+    live = act_ref[mine_rows, :] == 1
+    mel_wide = mel_ref[...].astype(jnp.float32)
+    for f in range(FRAMES + LOOK):
+        mel_t[f * rows : (f + 1) * rows, :] = mel_wide[:, f * MELS : (f + 1) * MELS]
     span = MELS
-    pre = jnp.dot(mel_ref[0 : FRAMES * rows, :], wpre_ref[0:span, :], preferred_element_type=jnp.float32)
+    pre = jnp.dot(
+        mel_t[0 : FRAMES * rows, :].astype(jnp.bfloat16), wpre_ref[0:span, :],
+        preferred_element_type=jnp.float32,
+    )
     for k in range(1, LOOK + 1):
         pre = pre + jnp.dot(
-            mel_ref[k * rows : (k + FRAMES) * rows, :],
+            mel_t[k * rows : (k + FRAMES) * rows, :].astype(jnp.bfloat16),
             wpre_ref[k * span : (k + 1) * span, :],
             preferred_element_type=jnp.float32,
         )
@@ -219,12 +250,11 @@
         wait_piece(sendbuf, new_ref, *OUT_PIECES[p], out_send, out_recv, out_local, p)
 
 
-def vocode_exchange(mel_rows, old_cache, picking, placing, live, w_pre, w_up, res_first, res_second):
+def vocode_exchange(mel_rows, old_cache, new_owner, prev_owner, live, w_pre, w_up, res_first, res_second):
     n = lax.axis_size("pool")
     rows = mel_rows.shape[0]
     slot_total, width = old_cache.shape
     length = UP * FRAMES
-    mel_t = mel_rows.reshape(rows, FRAMES + LOOK, MELS).transpose(1, 0, 2).reshape(-1, MELS)
     vmem = pl.BlockSpec(memory_space=pltpu.VMEM)
     anywhere = pl.BlockSpec(memory_space=pl.ANY)
     flops = 2 * rows * (FRAMES * (LOOK + 1) * MELS * C0 + FRAMES * 2 * C0 * UP * C1 + 6 * length * 3 * C1 * C1)
@@ -244,6 +274,9 @@
             pltpu.VMEM((length * rows, C1), jnp.float32),
             pltpu.VMEM(((length + 10) * rows, C1), jnp.bfloat16),
             pltpu.VMEM(((length + 2) * rows, C1), jnp.bfloat16),
+            pltpu.VMEM(((FRAMES + LOOK) * rows, MELS), jnp.float32),
+            pltpu.VMEM((rows, slot_total), jnp.bfloat16),
+            pltpu.VMEM((slot_total, rows), jnp.bfloat16),
             pltpu.SemaphoreType.DMA((len(IN_PIECES), n)),
             pltpu.SemaphoreType.DMA((len(IN_PIECES), n)),
             pltpu.SemaphoreType.DMA((len(IN_PIECES),)),
@@ -255,7 +288,7 @@
             collective_id=0, has_side_effects=True, vmem_limit_bytes=60 * 1024 * 1024
         ),
         cost_estimate=pl.CostEstimate(flops=flops, transcendentals=0, bytes_accessed=16 * 1024 * 1024),
-    )(mel_t, old_cache, picking, placing, live, w_pre, w_up, res_first, res_second)
+    )(mel_rows, old_cache, new_owner, prev_owner, live, w_pre, w_up, res_first, res_second)
 
 
 def ranks_of(owners):
@@ -268,23 +301,8 @@
 def on_device(
     mel_rows, old_cache, new_owner, prev_owner, active, w_pre, w_up, res_first, res_second
 ):
-    pool_size = lax.axis_size("pool")
-    position = lax.axis_index("pool")
-    rows_here = mel_rows.shape[0]
-    slot_total = old_cache.shape[0]
-    capacity = slot_total // pool_size
-    my_new = lax.dynamic_slice_in_dim(new_owner[:, 0], position * rows_here, rows_here)
-    my_prev = lax.dynamic_slice_in_dim(prev_owner[:, 0], position * rows_here, rows_here)
-    my_active = lax.dynamic_slice_in_dim(active, position * rows_here, rows_here)
-    my_new_rank = ranks_of(my_new[None])[0]
-    my_prev_rank = ranks_of(my_prev[None])[0]
-    picking = (
-        (my_prev * capacity + my_prev_rank)[:, None] == jnp.arange(slot_total)[None, :]
-    ).astype(jnp.bfloat16)
-    slot_ids = my_new * capacity + my_new_rank
-    placing = (jnp.arange(slot_total)[:, None] == slot_ids[None, :]).astype(jnp.bfloat16)
     return vocode_exchange(
-        mel_rows, old_cache, picking, placing, my_active[:, None], w_pre, w_up, res_first, res_second
+        mel_rows, old_cache, new_owner, prev_owner, active[:, None], w_pre, w_up, res_first, res_second
     )
 
 

time: 58.7 us -> 57.8 us (0.985)
  other arithmetic: 2.38 us -> 0 us
  local copies, waits for them, and re-layouts: 8.22 us -> 9.32 us
    unnamed x6, local copies, waits for them, and re-layouts: 4.88 us -> 7.62 us
    reshape x2 -> x0, local copies, waits for them, and re-layouts: 1.86 us -> none  [vocode_exchange(): mel_rows.reshape(rows, FRAMES + LOOK, MELS).transpose(1, 0, 2)]
    convert_element_type x2 -> x0, other arithmetic: 1.27 us -> none  [the longest x1 0.66 us: on_device(): picking = ((my_prev * capacity + my_prev_rank)[:, None] == jnp.arange(slo...]
    broadcast_in_dim x2 -> x1, local copies, waits for them, and re-layouts: 0.75 us -> 1.71 us  [on_device(): active[:, None]]
    eq x1 -> x0, other arithmetic: 0.75 us -> none  [on_device(): (my_prev * capacity + my_prev_rank)[:, None]]
    eq x1 -> x0, local copies, waits for them, and re-layouts: 0.73 us -> none  [ranks_of(): same_owner = owners[:, :, None] == owners[:, None, :]]
where the time goes in v4:
time: 57.8 us; the launch traced here: 57.6 us
  Pallas kernels  47.6 us (82%)
  local copies, waits for them, and re-layouts  9.32 us (16%)
  between operations  0.65 us (1%)
    pallas_call x1, Pallas kernels, vocode_exchange(): pl.pallas_call(fused_kernel, in_specs=[vmem, anywhere] + [vmem] * 7, out_...  47.6 us
    unnamed x6, local copies, waits for them, and re-layouts  7.62 us
    broadcast_in_dim x1, local copies, waits for them, and re-layouts, on_device(): active[:, None]  1.71 us

profile of v4, /device:TPU:1, one launch (start us, length us, event | category | flops | bytes accessed | tf_op | source)
XLA Modules:
  0.0 57.6 jit_solution(4347931743483526188)
XLA Ops:
  0.6 1.7 %copy.13.new_owner_ref = s32[1024,1]{1,0:T(8,128)} copy(s32[1024,1]{0,1:T(1,128)} %param.11) | data formatting | bytes 8192 | tf_op args[2]
  2.3 1.7 %copy.14.prev_owner_ref = s32[1024,1]{1,0:T(8,128)} copy(s32[1024,1]{0,1:T(1,128)} %param.12) | data formatting | bytes 8192 | tf_op args[3]
  4.0 1.7 %copy.15.act_ref = s32[1024,1]{1,0:T(8,128)} copy(s32[1024,1]{0,1:T(1,128)} %bitcast.1) | data formatting | bytes 8192 | tf_op jit(solution)/shard_map/broadcast_in_dim | solution.py:305
  5.8 47.6 %shard_map.104 = (bf16[32,36864]{1,0:T(8,128)(2,1)}, bf16[64,6656]{1,0:T(8,128)(2,1)}) custom-call(bf16[32,1920]{1,0:T(8,128)(2,1)} %mel_ref.1, bf16[64,6656]{1,0:T(8,128)(2,1)} %old_ref.1, s32[1024,1]{1,0:T(8,128)} %copy.13.new_owner_ref, s32[1024,1]{1,0:T(8,128)} %copy.14.prev_owner_ref, s32[1024,1]{1,0:T(8,128)} %copy.15.act_ref, ...), custom_call_target="tpu_custom_call" | custom-call | flops 13617856512 | bytes 16777216 | tf_op jit(solution)/shard_map/pallas_call | solution.py:261
  53.3 0.0 copy-start
  53.4 3.3 %copy.18 = bf16[32,36864]{1,0:T(8,128)(2,1)} copy(bf16[32,36864]{1,0:T(8,128)(2,1)} %get-tuple-element.4) | data formatting | bytes 4718592
  56.7 0.0 copy-done
  56.7 0.9 %copy.19 = bf16[64,6656]{1,0:T(8,128)(2,1)} copy(bf16[64,6656]{1,0:T(8,128)(2,1)S(1)} %copy-done) | data formatting | bytes 1703936
Async XLA Ops:
  53.3 3.3 %copy-start = (bf16[64,6656]{1,0:T(8,128)(2,1)S(1)}, bf16[64,6656]{1,0:T(8,128)(2,1)}, u32[]{:S(2)}) copy-start(bf16[64,6656]{1,0:T(8,128)(2,1)} %get-tuple-element.5) | copy-start | bytes 2555908

commit v5 on v4

--- a/solution.py
+++ b/solution.py
@@ -47,7 +47,7 @@
 
 
 def fused_kernel(
-    mel_ref, old_ref, new_owner_ref, prev_owner_ref, act_ref, wpre_ref, wup_ref, rf_ref, rs_ref,
+    mel_ref, old_ref, table_ref, wpre_ref, wup_ref, rf_ref, rs_ref,
     wave_ref, new_ref,
     arrived, sendbuf, held, kept, x_ref, a_ref, e_ref, mel_t, pick_ref, place_ref,
     in_send, in_recv, in_local, out_send, out_recv, out_local,
@@ -57,7 +57,6 @@
     rows = held.shape[0]
     length = UP * FRAMES
     me = lax.axis_index("pool")
-    mine_rows = pl.ds(pl.multiple_of(me * rows, rows), rows)
 
     barrier = pltpu.get_barrier_semaphore()
 
@@ -133,11 +132,11 @@
     start_piece(old_ref, arrived, *IN_PIECES[1], in_send, in_recv, in_local, 1)
 
     picking, placing = slot_tables(
-        new_owner_ref[mine_rows, :], prev_owner_ref[mine_rows, :], rows, old_ref.shape[0], cap
+        table_ref[:, 0:1], table_ref[:, 1:2], rows, old_ref.shape[0], cap
     )
     pick_ref[...] = picking
     place_ref[...] = placing
-    live = act_ref[mine_rows, :] == 1
+    live = table_ref[:, 2:3] == 1
     mel_wide = mel_ref[...].astype(jnp.float32)
     for f in range(FRAMES + LOOK):
         mel_t[f * rows : (f + 1) * rows, :] = mel_wide[:, f * MELS : (f + 1) * MELS]
@@ -250,7 +249,7 @@
         wait_piece(sendbuf, new_ref, *OUT_PIECES[p], out_send, out_recv, out_local, p)
 
 
-def vocode_exchange(mel_rows, old_cache, new_owner, prev_owner, live, w_pre, w_up, res_first, res_second):
+def vocode_exchange(mel_rows, old_cache, table, w_pre, w_up, res_first, res_second):
     n = lax.axis_size("pool")
     rows = mel_rows.shape[0]
     slot_total, width = old_cache.shape
@@ -260,7 +259,7 @@
     flops = 2 * rows * (FRAMES * (LOOK + 1) * MELS * C0 + FRAMES * 2 * C0 * UP * C1 + 6 * length * 3 * C1 * C1)
     return pl.pallas_call(
         fused_kernel,
-        in_specs=[vmem, anywhere] + [vmem] * 7,
+        in_specs=[vmem, anywhere] + [vmem] * 5,
         out_specs=[vmem, anywhere],
         out_shape=[
             jax.ShapeDtypeStruct((rows, length * C1), jnp.bfloat16),
@@ -288,7 +287,7 @@
             collective_id=0, has_side_effects=True, vmem_limit_bytes=60 * 1024 * 1024
         ),
         cost_estimate=pl.CostEstimate(flops=flops, transcendentals=0, bytes_accessed=16 * 1024 * 1024),
-    )(mel_rows, old_cache, new_owner, prev_owner, live, w_pre, w_up, res_first, res_second)
+    )(mel_rows, old_cache, table, w_pre, w_up, res_first, res_second)
 
 
 def ranks_of(owners):
@@ -301,9 +300,17 @@
 def on_device(
     mel_rows, old_cache, new_owner, prev_owner, active, w_pre, w_up, res_first, res_second
 ):
-    return vocode_exchange(
-        mel_rows, old_cache, new_owner, prev_owner, active[:, None], w_pre, w_up, res_first, res_second
-    )
+    rows = mel_rows.shape[0]
+    start = lax.axis_index("pool") * rows
+    table = jnp.concatenate(
+        [
+            lax.dynamic_slice_in_dim(new_owner, start, rows),
+            lax.dynamic_slice_in_dim(prev_owner, start, rows),
+            lax.dynamic_slice_in_dim(active, start, rows)[:, None],
+        ],
+        axis=1,
+    )
+    return vocode_exchange(mel_rows, old_cache, table, w_pre, w_up, res_first, res_second)
 
 
 def solution(mesh):

time: 57.8 us -> 54.4 us (0.941)
  local copies, waits for them, and re-layouts: 9.32 us -> 6.39 us
    unnamed x6, local copies, waits for them, and re-layouts: 7.62 us -> 4.88 us
    broadcast_in_dim x1, local copies, waits for them, and re-layouts: 1.71 us -> 0.07 us  [on_device(): lax.dynamic_slice_in_dim(active, start, rows)[:, None]]
    dynamic_slice x0 -> x1, local copies, waits for them, and re-layouts: none -> 0.74 us  [on_device(): lax.dynamic_slice_in_dim(prev_owner, start, rows)]
    concatenate x0 -> x1, local copies, waits for them, and re-layouts: none -> 0.69 us  [on_device(): jnp.concatenate([lax.dynamic_slice_in_dim(new_owner, start, rows), lax.dy...]
where the time goes in v5:
time: 54.4 us; the launch traced here: 54.2 us
  Pallas kernels  47.2 us (87%)
  local copies, waits for them, and re-layouts  6.39 us (12%)
  between operations  0.66 us (1%)
    pallas_call x1, Pallas kernels, vocode_exchange(): pl.pallas_call(fused_kernel, in_specs=[vmem, anywhere] + [vmem] * 5, out_...  47.2 us
    unnamed x6, local copies, waits for them, and re-layouts  4.88 us

profile of v5, /device:TPU:1, one launch (start us, length us, event | category | flops | bytes accessed | tf_op | source)
XLA Modules:
  0.0 54.2 jit_solution(3047649437337391739)
XLA Ops:
  0.6 0.0 copy-start
  0.6 0.7 %copy-done = s32[1024]{0:T(1024)S(1)} copy-done((s32[1024]{0:T(1024)S(1)}, s32[1024]{0:T(1024)}, u32[]{:S(2)}) %copy-start) | copy-done | bytes 4120
  1.3 0.1 dynamic-slice_bitcast_fusion
  1.4 0.7 %constant_dynamic-slice_fusion = (s32[32,1]{0,1:T(1,128)S(1)}, s32[32,1]{0,1:T(1,128)S(1)}) fusion(s32[1024,1]{0,1:T(1,128)} %param.12, s32[]{:T(128)S(6)} %select_n.2, s32[1024,1]{0,1:T(1,128)} %param.11), kind=kLoop, calls=%fused_computation.2 | loop fusion | bytes 516 | tf_op jit(solution)/shard_map/dynamic_slice | solution.py:308
  2.2 0.7 %copy.14.table_ref = s32[32,3]{1,0:T(8,128)} copy(s32[32,3]{0,1:T(4,128)S(1)} %pad_add_fusion) | data formatting | bytes 768 | tf_op jit(solution)/shard_map/concatenate | solution.py:305
  2.8 47.2 %shard_map.104 = (bf16[32,36864]{1,0:T(8,128)(2,1)}, bf16[64,6656]{1,0:T(8,128)(2,1)}) custom-call(bf16[32,1920]{1,0:T(8,128)(2,1)} %mel_ref.1, bf16[64,6656]{1,0:T(8,128)(2,1)} %old_ref.1, s32[32,3]{1,0:T(8,128)} %copy.14.table_ref, bf16[560,512]{1,0:T(8,128)(2,1)} %wpre_ref.1, bf16[1024,2048]{1,0:T(8,128)(2,1)} %wup_ref.1, bf16[3,768,256]{2,1,0:T(8,128)(2,1)} %rf_ref.1, ...), custom_call_target="tpu_custom_call" | custom-call | flops 13617856512 | bytes 16777216 | tf_op jit(solution)/shard_map/pallas_call | solution.py:260
  50.0 0.0 copy-start.1
  50.0 3.3 %copy.17 = bf16[32,36864]{1,0:T(8,128)(2,1)} copy(bf16[32,36864]{1,0:T(8,128)(2,1)} %get-tuple-element.6) | data formatting | bytes 4718592
  53.3 0.0 copy-done.1
  53.3 0.9 %copy.18 = bf16[64,6656]{1,0:T(8,128)(2,1)} copy(bf16[64,6656]{1,0:T(8,128)(2,1)S(1)} %copy-done.1) | data formatting | bytes 1703936
  (1 shorter events, 0.0 us)
Async XLA Ops:
  0.6 0.7 %copy-start = (s32[1024]{0:T(1024)S(1)}, s32[1024]{0:T(1024)}, u32[]{:S(2)}) copy-start(s32[1024]{0:T(1024)} %param.13) | copy-start | bytes 12292
  50.0 3.3 %copy-start.1 = (bf16[64,6656]{1,0:T(8,128)(2,1)S(1)}, bf16[64,6656]{1,0:T(8,128)(2,1)}, u32[]{:S(2)}) copy-start(bf16[64,6656]{1,0:T(8,128)(2,1)} %get-tuple-element.7) | copy-start | bytes 2555908

commit v6 on v5

--- a/solution.py
+++ b/solution.py
@@ -160,15 +160,19 @@
         )
         x_ref[pl.ds(j * rows, rows), :] = part[0:rows]
         for t in range(1, FRAMES):
-            x_ref[pl.ds((UP * t + j) * rows, rows), :] = (
-                part[t * rows : (t + 1) * rows] + rest[(t - 1) * rows : t * rows]
+            slab = part[t * rows : (t + 1) * rows] + rest[(t - 1) * rows : t * rows]
+            x_ref[pl.ds((UP * t + j) * rows, rows), :] = slab
+            a_ref[pl.ds((2 * DILATIONS[0] + UP * t + j) * rows, rows), :] = leaky_relu(slab).astype(
+                jnp.bfloat16
             )
 
     fetch(0)
     start_piece(old_ref, arrived, *IN_PIECES[2], in_send, in_recv, in_local, 2)
     head = jnp.dot(held[:, 0:C0], wup_ref[0:C0, :], preferred_element_type=jnp.float32)
     for j in range(UP):
-        x_ref[pl.ds(j * rows, rows), :] = x_ref[pl.ds(j * rows, rows), :] + head[:, j * C1 : (j + 1) * C1]
+        slab = x_ref[pl.ds(j * rows, rows), :] + head[:, j * C1 : (j + 1) * C1]
+        x_ref[pl.ds(j * rows, rows), :] = slab
+        a_ref[pl.ds((2 * DILATIONS[0] + j) * rows, rows), :] = leaky_relu(slab).astype(jnp.bfloat16)
     kept[:, 0:C0] = jnp.where(live, pre_act[(FRAMES - 1) * rows :], held[:, 0:C0])
 
     offset = C0
@@ -192,7 +196,6 @@
             ).astype(jnp.bfloat16)
             return carry
 
-        lax.fori_loop(0, steps, fill, 0)
         for p in range(2 * dilation):
             kept[:, a_off + p * C1 : a_off + (p + 1) * C1] = jnp.where(
                 live,
@@ -238,13 +241,24 @@
                     preferred_element_type=jnp.float32,
                 )
             x_ref[pl.ds(r, CHUNK), :] = z
-            return carry
-
-        lax.fori_loop(0, steps, second, 0)
-    for m in range(length):
-        wave_ref[:, m * C1 : (m + 1) * C1] = jnp.where(
-            live, x_ref[pl.ds(m * rows, rows), :], 0.0
-        ).astype(jnp.bfloat16)
+            if section + 1 < len(DILATIONS):
+                ahead = 2 * DILATIONS[section + 1] * rows
+                a_ref[pl.ds(pl.multiple_of(ahead + r, 16), CHUNK), :] = leaky_relu(z).astype(
+                    jnp.bfloat16
+                )
+            return carry
+
+        if section + 1 < len(DILATIONS):
+            lax.fori_loop(0, steps, second, 0)
+        else:
+            for c in range(steps):
+                second(c, 0)
+                z = x_ref[c * CHUNK : (c + 1) * CHUNK, :]
+                for m in range(CHUNK // rows):
+                    sample = c * CHUNK // rows + m
+                    wave_ref[:, sample * C1 : (sample + 1) * C1] = jnp.where(
+                        live, z[m * rows : (m + 1) * rows], 0.0
+                    ).astype(jnp.bfloat16)
     for p in range(len(OUT_PIECES)):
         wait_piece(sendbuf, new_ref, *OUT_PIECES[p], out_send, out_recv, out_local, p)
 

time: 54.4 us -> 52.4 us (0.963)
  Pallas kernels: 47.2 us -> 45.2 us
    pallas_call x1, Pallas kernels: 47.2 us -> 45.2 us  [vocode_exchange(): pl.pallas_call(fused_kernel, in_specs=[vmem, anywhere] + [vmem] * 5, out_...]
where the time goes in v6:
time: 52.4 us; the launch traced here: 52.2 us
  Pallas kernels  45.2 us (86%)
  local copies, waits for them, and re-layouts  6.39 us (12%)
  between operations  0.66 us (1%)
    pallas_call x1, Pallas kernels, vocode_exchange(): pl.pallas_call(fused_kernel, in_specs=[vmem, anywhere] + [vmem] * 5, out_...  45.2 us
    unnamed x6, local copies, waits for them, and re-layouts  4.88 us

profile of v6, /device:TPU:1, one launch (start us, length us, event | category | flops | bytes accessed | tf_op | source)
XLA Modules:
  0.0 52.2 jit_solution(1869920718300392975)
XLA Ops:
  0.6 0.0 copy-start
  0.6 0.7 %copy-done = s32[1024]{0:T(1024)S(1)} copy-done((s32[1024]{0:T(1024)S(1)}, s32[1024]{0:T(1024)}, u32[]{:S(2)}) %copy-start) | copy-done | bytes 4120
  1.3 0.1 dynamic-slice_bitcast_fusion
  1.4 0.7 %constant_dynamic-slice_fusion = (s32[32,1]{0,1:T(1,128)S(1)}, s32[32,1]{0,1:T(1,128)S(1)}) fusion(s32[1024,1]{0,1:T(1,128)} %param.12, s32[]{:T(128)S(6)} %select_n.2, s32[1024,1]{0,1:T(1,128)} %param.11), kind=kLoop, calls=%fused_computation.2 | loop fusion | bytes 516 | tf_op jit(solution)/shard_map/dynamic_slice | solution.py:322
  2.2 0.7 %copy.14.table_ref = s32[32,3]{1,0:T(8,128)} copy(s32[32,3]{0,1:T(4,128)S(1)} %pad_add_fusion) | data formatting | bytes 768 | tf_op jit(solution)/shard_map/concatenate | solution.py:319
  2.8 45.2 %shard_map.104 = (bf16[32,36864]{1,0:T(8,128)(2,1)}, bf16[64,6656]{1,0:T(8,128)(2,1)}) custom-call(bf16[32,1920]{1,0:T(8,128)(2,1)} %mel_ref.1, bf16[64,6656]{1,0:T(8,128)(2,1)} %old_ref.1, s32[32,3]{1,0:T(8,128)} %copy.14.table_ref, bf16[560,512]{1,0:T(8,128)(2,1)} %wpre_ref.1, bf16[1024,2048]{1,0:T(8,128)(2,1)} %wup_ref.1, bf16[3,768,256]{2,1,0:T(8,128)(2,1)} %rf_ref.1, ...), custom_call_target="tpu_custom_call" | custom-call | flops 13617856512 | bytes 16777216 | tf_op jit(solution)/shard_map/pallas_call | solution.py:274
  48.0 0.0 copy-start.1
  48.0 3.3 %copy.17 = bf16[32,36864]{1,0:T(8,128)(2,1)} copy(bf16[32,36864]{1,0:T(8,128)(2,1)} %get-tuple-element.6) | data formatting | bytes 4718592
  51.3 0.0 copy-done.1
  51.3 0.9 %copy.18 = bf16[64,6656]{1,0:T(8,128)(2,1)} copy(bf16[64,6656]{1,0:T(8,128)(2,1)S(1)} %copy-done.1) | data formatting | bytes 1703936
  (1 shorter events, 0.0 us)
Async XLA Ops:
  0.6 0.7 %copy-start = (s32[1024]{0:T(1024)S(1)}, s32[1024]{0:T(1024)}, u32[]{:S(2)}) copy-start(s32[1024]{0:T(1024)} %param.13) | copy-start | bytes 12292
  48.0 3.3 %copy-start.1 = (bf16[64,6656]{1,0:T(8,128)(2,1)S(1)}, bf16[64,6656]{1,0:T(8,128)(2,1)}, u32[]{:S(2)}) copy-start(bf16[64,6656]{1,0:T(8,128)(2,1)} %get-tuple-element.7) | copy-start | bytes 2555908

commit v7 on v6

--- a/solution.py
+++ b/solution.py
@@ -27,12 +27,24 @@
 OUT_PIECES = ((0, 1536), (1536, 3584), (3584, 6144), (6144, 6656))
 
 
-def slot_tables(new_col, prev_col, rows, slots, cap):
+def slot_tables(new_ref, prev_ref, act_ref, base, rows, slots, cap):
+    column = lax.broadcasted_iota(jnp.int32, (rows, 1), 0)
+    row = lax.broadcasted_iota(jnp.int32, (1, rows), 1)
+    new_col = jnp.zeros((rows, 1), jnp.int32)
+    new_row = jnp.zeros((1, rows), jnp.int32)
+    prev_col = jnp.zeros((rows, 1), jnp.int32)
+    prev_row = jnp.zeros((1, rows), jnp.int32)
+    act_col = jnp.zeros((rows, 1), jnp.int32)
+    for u in range(rows):
+        new_u = new_ref[base + u]
+        prev_u = prev_ref[base + u]
+        new_col = jnp.where(column == u, new_u, new_col)
+        new_row = jnp.where(row == u, new_u, new_row)
+        prev_col = jnp.where(column == u, prev_u, prev_col)
+        prev_row = jnp.where(row == u, prev_u, prev_row)
+        act_col = jnp.where(column == u, act_ref[base + u], act_col)
     ids = lax.broadcasted_iota(jnp.int32, (rows, rows), 0)
     other = lax.broadcasted_iota(jnp.int32, (rows, rows), 1)
-    diagonal = ids == other
-    new_row = jnp.sum(jnp.where(diagonal, new_col, 0), axis=0, keepdims=True)
-    prev_row = jnp.sum(jnp.where(diagonal, prev_col, 0), axis=0, keepdims=True)
     prev_rank = jnp.sum(
         jnp.where((prev_col == prev_row) & (other < ids), 1, 0), axis=1, keepdims=True
     )
@@ -43,11 +55,11 @@
     placing = (
         lax.broadcasted_iota(jnp.int32, (slots, rows), 0) == new_row * cap + new_rank
     ).astype(jnp.bfloat16)
-    return picking, placing
+    return picking, placing, act_col == 1
 
 
 def fused_kernel(
-    mel_ref, old_ref, table_ref, wpre_ref, wup_ref, rf_ref, rs_ref,
+    mel_ref, old_ref, new_owner_ref, prev_owner_ref, active_ref, wpre_ref, wup_ref, rf_ref, rs_ref,
     wave_ref, new_ref,
     arrived, sendbuf, held, kept, x_ref, a_ref, e_ref, mel_t, pick_ref, place_ref,
     in_send, in_recv, in_local, out_send, out_recv, out_local,
@@ -72,7 +84,8 @@
         mine = pl.ds(pl.multiple_of(me * cap, cap), cap)
         pltpu.make_async_copy(src.at[mine, cols], dst.at[mine, cols], locals_.at[p]).start()
 
-        def body(s, carry):
+        def body(i, carry):
+            s = n - i
             peer = lax.rem(me + s, n)
             pltpu.make_async_remote_copy(
                 src_ref=src.at[pl.ds(pl.multiple_of(peer * cap, cap), cap), cols],
@@ -131,12 +144,11 @@
     start_piece(old_ref, arrived, *IN_PIECES[0], in_send, in_recv, in_local, 0)
     start_piece(old_ref, arrived, *IN_PIECES[1], in_send, in_recv, in_local, 1)
 
-    picking, placing = slot_tables(
-        table_ref[:, 0:1], table_ref[:, 1:2], rows, old_ref.shape[0], cap
+    picking, placing, live = slot_tables(
+        new_owner_ref, prev_owner_ref, active_ref, me * rows, rows, old_ref.shape[0], cap
     )
     pick_ref[...] = picking
     place_ref[...] = placing
-    live = table_ref[:, 2:3] == 1
     mel_wide = mel_ref[...].astype(jnp.float32)
     for f in range(FRAMES + LOOK):
         mel_t[f * rows : (f + 1) * rows, :] = mel_wide[:, f * MELS : (f + 1) * MELS]
@@ -263,17 +275,18 @@
         wait_piece(sendbuf, new_ref, *OUT_PIECES[p], out_send, out_recv, out_local, p)
 
 
-def vocode_exchange(mel_rows, old_cache, table, w_pre, w_up, res_first, res_second):
+def vocode_exchange(mel_rows, old_cache, new_owner, prev_owner, active, w_pre, w_up, res_first, res_second):
     n = lax.axis_size("pool")
     rows = mel_rows.shape[0]
     slot_total, width = old_cache.shape
     length = UP * FRAMES
     vmem = pl.BlockSpec(memory_space=pltpu.VMEM)
     anywhere = pl.BlockSpec(memory_space=pl.ANY)
+    smem = pl.BlockSpec(memory_space=pltpu.SMEM)
     flops = 2 * rows * (FRAMES * (LOOK + 1) * MELS * C0 + FRAMES * 2 * C0 * UP * C1 + 6 * length * 3 * C1 * C1)
     return pl.pallas_call(
         fused_kernel,
-        in_specs=[vmem, anywhere] + [vmem] * 5,
+        in_specs=[vmem, anywhere] + [smem] * 3 + [vmem] * 4,
         out_specs=[vmem, anywhere],
         out_shape=[
             jax.ShapeDtypeStruct((rows, length * C1), jnp.bfloat16),
@@ -301,7 +314,7 @@
             collective_id=0, has_side_effects=True, vmem_limit_bytes=60 * 1024 * 1024
         ),
         cost_estimate=pl.CostEstimate(flops=flops, transcendentals=0, bytes_accessed=16 * 1024 * 1024),
-    )(mel_rows, old_cache, table, w_pre, w_up, res_first, res_second)
+    )(mel_rows, old_cache, new_owner, prev_owner, active, w_pre, w_up, res_first, res_second)
 
 
 def ranks_of(owners):
@@ -314,17 +327,9 @@
 def on_device(
     mel_rows, old_cache, new_owner, prev_owner, active, w_pre, w_up, res_first, res_second
 ):
-    rows = mel_rows.shape[0]
-    start = lax.axis_index("pool") * rows
-    table = jnp.concatenate(
-        [
-            lax.dynamic_slice_in_dim(new_owner, start, rows),
-            lax.dynamic_slice_in_dim(prev_owner, start, rows),
-            lax.dynamic_slice_in_dim(active, start, rows)[:, None],
-        ],
-        axis=1,
-    )
-    return vocode_exchange(mel_rows, old_cache, table, w_pre, w_up, res_first, res_second)
+    return vocode_exchange(
+        mel_rows, old_cache, new_owner[:, 0], prev_owner[:, 0], active, w_pre, w_up, res_first, res_second
+    )
 
 
 def solution(mesh):

time: 52.4 us -> 50.3 us (0.960)
  local copies, waits for them, and re-layouts: 6.39 us -> 4.2 us
    dynamic_slice x1 -> x0, local copies, waits for them, and re-layouts: 0.74 us -> none  [on_device(): lax.dynamic_slice_in_dim(prev_owner, start, rows)]
    concatenate x1 -> x0, local copies, waits for them, and re-layouts: 0.69 us -> none  [on_device(): jnp.concatenate([lax.dynamic_slice_in_dim(new_owner, start, rows), lax.dy...]
    unnamed x6 -> x4, local copies, waits for them, and re-layouts: 4.88 us -> 4.2 us
where the time goes in v7:
time: 50.3 us; the launch traced here: 50.1 us
  Pallas kernels  45.3 us (90%)
  local copies, waits for them, and re-layouts  4.2 us (8%)
  between operations  0.65 us (1%)
    pallas_call x1, Pallas kernels, vocode_exchange(): pl.pallas_call(fused_kernel, in_specs=[vmem, anywhere] + [smem] * 3 + [vm...  45.3 us
    unnamed x4, local copies, waits for them, and re-layouts  4.2 us

profile of v7, /device:TPU:1, one launch (start us, length us, event | category | flops | bytes accessed | tf_op | source)
XLA Modules:
  0.0 50.1 jit_solution(9653751341433396251)
XLA Ops:
  0.6 45.3 %shard_map.104 = (bf16[32,36864]{1,0:T(8,128)(2,1)}, bf16[64,6656]{1,0:T(8,128)(2,1)}) custom-call(bf16[32,1920]{1,0:T(8,128)(2,1)} %mel_ref.1, bf16[64,6656]{1,0:T(8,128)(2,1)} %old_ref.1, s32[1024]{0:T(1024)} %bitcast.2, s32[1024]{0:T(1024)} %bitcast.3, s32[1024]{0:T(1024)} %active_ref.1, bf16[560,512]{1,0:T(8,128)(2,1)} %wpre_ref.1, ...), custom_call_target="tpu_custom_call" | custom-call | flops 13617856512 | bytes 16777216 | tf_op jit(solution)/shard_map/pallas_call | solution.py:287
  45.9 0.0 copy-start
  45.9 3.3 %copy.13 = bf16[32,36864]{1,0:T(8,128)(2,1)} copy(bf16[32,36864]{1,0:T(8,128)(2,1)} %get-tuple-element.4) | data formatting | bytes 4718592
  49.2 0.0 copy-done
  49.2 0.9 %copy.14 = bf16[64,6656]{1,0:T(8,128)(2,1)} copy(bf16[64,6656]{1,0:T(8,128)(2,1)S(1)} %copy-done) | data formatting | bytes 1703936
Async XLA Ops:
  45.9 3.3 %copy-start = (bf16[64,6656]{1,0:T(8,128)(2,1)S(1)}, bf16[64,6656]{1,0:T(8,128)(2,1)}, u32[]{:S(2)}) copy-start(bf16[64,6656]{1,0:T(8,128)(2,1)} %get-tuple-element.5) | copy-start | bytes 2555908

commit v8 on v7

--- a/solution.py
+++ b/solution.py
@@ -15,7 +15,7 @@
 
 DILATIONS = (1, 3, 5)
 SLOPE = 0.1
-CHUNK = 768
+CHUNK = 2304
 
 
 def leaky_relu(values):

time: 50.3 us -> 46.8 us (0.930)
  Pallas kernels: 45.3 us -> 41.9 us
    pallas_call x1, Pallas kernels: 45.3 us -> 41.9 us  [vocode_exchange(): pl.pallas_call(fused_kernel, in_specs=[vmem, anywhere] + [smem] * 3 + [vm...]
where the time goes in v8:
time: 46.8 us; the launch traced here: 46.7 us
  Pallas kernels  41.9 us (90%)
  local copies, waits for them, and re-layouts  4.2 us (9%)
  between operations  0.65 us (1%)
    pallas_call x1, Pallas kernels, vocode_exchange(): pl.pallas_call(fused_kernel, in_specs=[vmem, anywhere] + [smem] * 3 + [vm...  41.9 us
    unnamed x4, local copies, waits for them, and re-layouts  4.2 us

profile of v8, /device:TPU:1, one launch (start us, length us, event | category | flops | bytes accessed | tf_op | source)
XLA Modules:
  0.0 46.7 jit_solution(11361729702555700359)
XLA Ops:
  0.6 41.9 %shard_map.104 = (bf16[32,36864]{1,0:T(8,128)(2,1)}, bf16[64,6656]{1,0:T(8,128)(2,1)}) custom-call(bf16[32,1920]{1,0:T(8,128)(2,1)} %mel_ref.1, bf16[64,6656]{1,0:T(8,128)(2,1)} %old_ref.1, s32[1024]{0:T(1024)} %bitcast.2, s32[1024]{0:T(1024)} %bitcast.3, s32[1024]{0:T(1024)} %active_ref.1, bf16[560,512]{1,0:T(8,128)(2,1)} %wpre_ref.1, ...), custom_call_target="tpu_custom_call" | custom-call | flops 13617856512 | bytes 16777216 | tf_op jit(solution)/shard_map/pallas_call | solution.py:287
  42.5 0.0 copy-start
  42.5 3.3 %copy.13 = bf16[32,36864]{1,0:T(8,128)(2,1)} copy(bf16[32,36864]{1,0:T(8,128)(2,1)} %get-tuple-element.4) | data formatting | bytes 4718592
  45.8 0.0 copy-done
  45.8 0.9 %copy.14 = bf16[64,6656]{1,0:T(8,128)(2,1)} copy(bf16[64,6656]{1,0:T(8,128)(2,1)S(1)} %copy-done) | data formatting | bytes 1703936
Async XLA Ops:
  42.5 3.3 %copy-start = (bf16[64,6656]{1,0:T(8,128)(2,1)S(1)}, bf16[64,6656]{1,0:T(8,128)(2,1)}, u32[]{:S(2)}) copy-start(bf16[64,6656]{1,0:T(8,128)(2,1)} %get-tuple-element.5) | copy-start | bytes 2555908

commit v9 on v8

--- a/solution.py
+++ b/solution.py
@@ -143,6 +143,7 @@
 
     start_piece(old_ref, arrived, *IN_PIECES[0], in_send, in_recv, in_local, 0)
     start_piece(old_ref, arrived, *IN_PIECES[1], in_send, in_recv, in_local, 1)
+    start_piece(old_ref, arrived, *IN_PIECES[2], in_send, in_recv, in_local, 2)
 
     picking, placing, live = slot_tables(
         new_owner_ref, prev_owner_ref, active_ref, me * rows, rows, old_ref.shape[0], cap
@@ -179,7 +180,6 @@
             )
 
     fetch(0)
-    start_piece(old_ref, arrived, *IN_PIECES[2], in_send, in_recv, in_local, 2)
     head = jnp.dot(held[:, 0:C0], wup_ref[0:C0, :], preferred_element_type=jnp.float32)
     for j in range(UP):
         slab = x_ref[pl.ds(j * rows, rows), :] + head[:, j * C1 : (j + 1) * C1]

time: 46.8 us -> 46.3 us (0.989)
  Pallas kernels: 41.9 us -> 41.3 us
    pallas_call x1, Pallas kernels: 41.9 us -> 41.3 us  [vocode_exchange(): pl.pallas_call(fused_kernel, in_specs=[vmem, anywhere] + [smem] * 3 + [vm...]
where the time goes in v9:
time: 46.3 us; the launch traced here: 46.2 us
  Pallas kernels  41.3 us (89%)
  local copies, waits for them, and re-layouts  4.2 us (9%)
  between operations  0.65 us (1%)
    pallas_call x1, Pallas kernels, vocode_exchange(): pl.pallas_call(fused_kernel, in_specs=[vmem, anywhere] + [smem] * 3 + [vm...  41.3 us
    unnamed x4, local copies, waits for them, and re-layouts  4.2 us

profile of v9, /device:TPU:1, one launch (start us, length us, event | category | flops | bytes accessed | tf_op | source)
XLA Modules:
  0.0 46.2 jit_solution(16837281644727699109)
XLA Ops:
  0.6 41.3 %shard_map.104 = (bf16[32,36864]{1,0:T(8,128)(2,1)}, bf16[64,6656]{1,0:T(8,128)(2,1)}) custom-call(bf16[32,1920]{1,0:T(8,128)(2,1)} %mel_ref.1, bf16[64,6656]{1,0:T(8,128)(2,1)} %old_ref.1, s32[1024]{0:T(1024)} %bitcast.2, s32[1024]{0:T(1024)} %bitcast.3, s32[1024]{0:T(1024)} %active_ref.1, bf16[560,512]{1,0:T(8,128)(2,1)} %wpre_ref.1, ...), custom_call_target="tpu_custom_call" | custom-call | flops 13617856512 | bytes 16777216 | tf_op jit(solution)/shard_map/pallas_call | solution.py:287
  42.0 0.0 copy-start
  42.0 3.3 %copy.13 = bf16[32,36864]{1,0:T(8,128)(2,1)} copy(bf16[32,36864]{1,0:T(8,128)(2,1)} %get-tuple-element.4) | data formatting | bytes 4718592
  45.3 0.0 copy-done
  45.3 0.9 %copy.14 = bf16[64,6656]{1,0:T(8,128)(2,1)} copy(bf16[64,6656]{1,0:T(8,128)(2,1)S(1)} %copy-done) | data formatting | bytes 1703936
Async XLA Ops:
  42.0 3.3 %copy-start = (bf16[64,6656]{1,0:T(8,128)(2,1)S(1)}, bf16[64,6656]{1,0:T(8,128)(2,1)}, u32[]{:S(2)}) copy-start(bf16[64,6656]{1,0:T(8,128)(2,1)} %get-tuple-element.5) | copy-start | bytes 2555908

commit v10 on v9

--- a/solution.py
+++ b/solution.py
@@ -59,11 +59,20 @@
 
 
 def fused_kernel(
-    mel_ref, old_ref, new_owner_ref, prev_owner_ref, active_ref, wpre_ref, wup_ref, rf_ref, rs_ref,
+    mel_ref, old_ref, new_owner_ref, prev_owner_ref, active_ref, wpre_hbm, wup_hbm, rf_hbm, rs_hbm,
     wave_ref, new_ref,
     arrived, sendbuf, held, kept, x_ref, a_ref, e_ref, mel_t, pick_ref, place_ref,
+    wpre_ref, wup_ref, rf_ref, rs_ref, weight_sem,
     in_send, in_recv, in_local, out_send, out_recv, out_local,
 ):
+    loads = [
+        pltpu.make_async_copy(source, target, weight_sem.at[i])
+        for i, (source, target) in enumerate(
+            ((wpre_hbm, wpre_ref), (wup_hbm, wup_ref), (rf_hbm, rf_ref), (rs_hbm, rs_ref))
+        )
+    ]
+    for load in loads:
+        load.start()
     n = in_send.shape[1]
     cap = old_ref.shape[0] // n
     rows = held.shape[0]
@@ -154,6 +163,7 @@
     for f in range(FRAMES + LOOK):
         mel_t[f * rows : (f + 1) * rows, :] = mel_wide[:, f * MELS : (f + 1) * MELS]
     span = MELS
+    loads[0].wait()
     pre = jnp.dot(
         mel_t[0 : FRAMES * rows, :].astype(jnp.bfloat16), wpre_ref[0:span, :],
         preferred_element_type=jnp.float32,
@@ -165,6 +175,7 @@
             preferred_element_type=jnp.float32,
         )
     pre_act = leaky_relu(pre).astype(jnp.bfloat16)
+    loads[1].wait()
     for j in range(UP):
         cols = slice(j * C1, (j + 1) * C1)
         part = jnp.dot(pre_act, wup_ref[C0 : 2 * C0, cols], preferred_element_type=jnp.float32)
@@ -187,6 +198,8 @@
         a_ref[pl.ds((2 * DILATIONS[0] + j) * rows, rows), :] = leaky_relu(slab).astype(jnp.bfloat16)
     kept[:, 0:C0] = jnp.where(live, pre_act[(FRAMES - 1) * rows :], held[:, 0:C0])
 
+    loads[2].wait()
+    loads[3].wait()
     offset = C0
     steps = length * rows // CHUNK
     for section, dilation in enumerate(DILATIONS):
@@ -286,7 +299,7 @@
     flops = 2 * rows * (FRAMES * (LOOK + 1) * MELS * C0 + FRAMES * 2 * C0 * UP * C1 + 6 * length * 3 * C1 * C1)
     return pl.pallas_call(
         fused_kernel,
-        in_specs=[vmem, anywhere] + [smem] * 3 + [vmem] * 4,
+        in_specs=[vmem, anywhere] + [smem] * 3 + [anywhere] * 4,
         out_specs=[vmem, anywhere],
         out_shape=[
             jax.ShapeDtypeStruct((rows, length * C1), jnp.bfloat16),
@@ -303,6 +316,11 @@
             pltpu.VMEM(((FRAMES + LOOK) * rows, MELS), jnp.float32),
             pltpu.VMEM((rows, slot_total), jnp.bfloat16),
             pltpu.VMEM((slot_total, rows), jnp.bfloat16),
+            pltpu.VMEM(w_pre.shape, w_pre.dtype),
+            pltpu.VMEM(w_up.shape, w_up.dtype),
+            pltpu.VMEM(res_first.shape, res_first.dtype),
+            pltpu.VMEM(res_second.shape, res_second.dtype),
+            pltpu.SemaphoreType.DMA((4,)),
             pltpu.SemaphoreType.DMA((len(IN_PIECES), n)),
             pltpu.SemaphoreType.DMA((len(IN_PIECES), n)),
             pltpu.SemaphoreType.DMA((len(IN_PIECES),)),

time: 46.3 us -> 44.3 us (0.957)
  Pallas kernels: 41.3 us -> 39.3 us
    pallas_call x1, Pallas kernels: 41.3 us -> 39.3 us  [vocode_exchange(): pl.pallas_call(fused_kernel, in_specs=[vmem, anywhere] + [smem] * 3 + [an...]
where the time goes in v10:
time: 44.3 us; the launch traced here: 44.1 us
  Pallas kernels  39.3 us (89%)
  local copies, waits for them, and re-layouts  4.2 us (9%)
  between operations  0.65 us (1%)
    pallas_call x1, Pallas kernels, vocode_exchange(): pl.pallas_call(fused_kernel, in_specs=[vmem, anywhere] + [smem] * 3 + [an...  39.3 us
    unnamed x4, local copies, waits for them, and re-layouts  4.2 us

profile of v10, /device:TPU:1, one launch (start us, length us, event | category | flops | bytes accessed | tf_op | source)
XLA Modules:
  0.0 44.1 jit_solution(15131130346656818983)
XLA Ops:
  0.6 39.3 %shard_map.104 = (bf16[32,36864]{1,0:T(8,128)(2,1)}, bf16[64,6656]{1,0:T(8,128)(2,1)}) custom-call(bf16[32,1920]{1,0:T(8,128)(2,1)} %mel_ref.1, bf16[64,6656]{1,0:T(8,128)(2,1)} %old_ref.1, s32[1024]{0:T(1024)} %bitcast.2, s32[1024]{0:T(1024)} %bitcast.3, s32[1024]{0:T(1024)} %active_ref.1, bf16[560,512]{1,0:T(8,128)(2,1)} %wpre_hbm.1, ...), custom_call_target="tpu_custom_call" | custom-call | flops 13617856512 | bytes 16777216 | tf_op jit(solution)/shard_map/pallas_call | solution.py:300
  39.9 0.0 copy-start
  39.9 3.3 %copy.13 = bf16[32,36864]{1,0:T(8,128)(2,1)} copy(bf16[32,36864]{1,0:T(8,128)(2,1)} %get-tuple-element.4) | data formatting | bytes 4718592
  43.2 0.0 copy-done
  43.2 0.9 %copy.14 = bf16[64,6656]{1,0:T(8,128)(2,1)} copy(bf16[64,6656]{1,0:T(8,128)(2,1)S(1)} %copy-done) | data formatting | bytes 1703936
Async XLA Ops:
  39.9 3.3 %copy-start = (bf16[64,6656]{1,0:T(8,128)(2,1)S(1)}, bf16[64,6656]{1,0:T(8,128)(2,1)}, u32[]{:S(2)}) copy-start(bf16[64,6656]{1,0:T(8,128)(2,1)} %get-tuple-element.5) | copy-start | bytes 2555908

commit v11 on v10

--- a/solution.py
+++ b/solution.py
@@ -60,9 +60,9 @@
 
 def fused_kernel(
     mel_ref, old_ref, new_owner_ref, prev_owner_ref, active_ref, wpre_hbm, wup_hbm, rf_hbm, rs_hbm,
-    wave_ref, new_ref,
+    wave_hbm, new_ref,
     arrived, sendbuf, held, kept, x_ref, a_ref, e_ref, mel_t, pick_ref, place_ref,
-    wpre_ref, wup_ref, rf_ref, rs_ref, weight_sem,
+    wpre_ref, wup_ref, rf_ref, rs_ref, weight_sem, wave_v, wave_sem,
     in_send, in_recv, in_local, out_send, out_recv, out_local,
 ):
     loads = [
@@ -202,6 +202,7 @@
     loads[3].wait()
     offset = C0
     steps = length * rows // CHUNK
+    stores = []
     for section, dilation in enumerate(DILATIONS):
         if section > 0:
             fetch(section)
@@ -281,11 +282,20 @@
                 z = x_ref[c * CHUNK : (c + 1) * CHUNK, :]
                 for m in range(CHUNK // rows):
                     sample = c * CHUNK // rows + m
-                    wave_ref[:, sample * C1 : (sample + 1) * C1] = jnp.where(
+                    wave_v[:, sample * C1 : (sample + 1) * C1] = jnp.where(
                         live, z[m * rows : (m + 1) * rows], 0.0
                     ).astype(jnp.bfloat16)
+                span_cols = pl.ds(c * CHUNK // rows * C1, CHUNK // rows * C1)
+                stores.append(
+                    pltpu.make_async_copy(
+                        wave_v.at[:, span_cols], wave_hbm.at[:, span_cols], wave_sem.at[c]
+                    )
+                )
+                stores[-1].start()
     for p in range(len(OUT_PIECES)):
         wait_piece(sendbuf, new_ref, *OUT_PIECES[p], out_send, out_recv, out_local, p)
+    for store in stores:
+        store.wait()
 
 
 def vocode_exchange(mel_rows, old_cache, new_owner, prev_owner, active, w_pre, w_up, res_first, res_second):
@@ -300,7 +310,7 @@
     return pl.pallas_call(
         fused_kernel,
         in_specs=[vmem, anywhere] + [smem] * 3 + [anywhere] * 4,
-        out_specs=[vmem, anywhere],
+        out_specs=[anywhere, anywhere],
         out_shape=[
             jax.ShapeDtypeStruct((rows, length * C1), jnp.bfloat16),
             jax.ShapeDtypeStruct((slot_total, width), jnp.bfloat16),
@@ -321,6 +331,8 @@
             pltpu.VMEM(res_first.shape, res_first.dtype),
             pltpu.VMEM(res_second.shape, res_second.dtype),
             pltpu.SemaphoreType.DMA((4,)),
+            pltpu.VMEM((rows, length * C1), jnp.bfloat16),
+            pltpu.SemaphoreType.DMA((length * rows // CHUNK,)),
             pltpu.SemaphoreType.DMA((len(IN_PIECES), n)),
             pltpu.SemaphoreType.DMA((len(IN_PIECES), n)),
             pltpu.SemaphoreType.DMA((len(IN_PIECES),)),

time: 44.3 us -> 42.9 us (0.968)
  Pallas kernels: 39.3 us -> 37.9 us
    pallas_call x1, Pallas kernels: 39.3 us -> 37.9 us  [vocode_exchange(): pl.pallas_call(fused_kernel, in_specs=[vmem, anywhere] + [smem] * 3 + [an...]
where the time goes in v11:
time: 42.9 us; the launch traced here: 42.7 us
  Pallas kernels  37.9 us (88%)
  local copies, waits for them, and re-layouts  4.2 us (10%)
  between operations  0.65 us (2%)
    pallas_call x1, Pallas kernels, vocode_exchange(): pl.pallas_call(fused_kernel, in_specs=[vmem, anywhere] + [smem] * 3 + [an...  37.9 us
    unnamed x4, local copies, waits for them, and re-layouts  4.2 us

profile of v11, /device:TPU:1, one launch (start us, length us, event | category | flops | bytes accessed | tf_op | source)
XLA Modules:
  0.0 42.7 jit_solution(15777116094001193723)
XLA Ops:
  0.6 37.9 %shard_map.104 = (bf16[32,36864]{1,0:T(8,128)(2,1)}, bf16[64,6656]{1,0:T(8,128)(2,1)}) custom-call(bf16[32,1920]{1,0:T(8,128)(2,1)} %mel_ref.1, bf16[64,6656]{1,0:T(8,128)(2,1)} %old_ref.1, s32[1024]{0:T(1024)} %bitcast.2, s32[1024]{0:T(1024)} %bitcast.3, s32[1024]{0:T(1024)} %active_ref.1, bf16[560,512]{1,0:T(8,128)(2,1)} %wpre_hbm.1, ...), custom_call_target="tpu_custom_call" | custom-call | flops 13617856512 | bytes 16777216 | tf_op jit(solution)/shard_map/pallas_call | solution.py:310
  38.5 0.0 copy-start
  38.5 3.3 %copy.13 = bf16[32,36864]{1,0:T(8,128)(2,1)} copy(bf16[32,36864]{1,0:T(8,128)(2,1)} %get-tuple-element.4) | data formatting | bytes 4718592
  41.8 0.0 copy-done
  41.8 0.9 %copy.14 = bf16[64,6656]{1,0:T(8,128)(2,1)} copy(bf16[64,6656]{1,0:T(8,128)(2,1)S(1)} %copy-done) | data formatting | bytes 1703936
Async XLA Ops:
  38.5 3.3 %copy-start = (bf16[64,6656]{1,0:T(8,128)(2,1)S(1)}, bf16[64,6656]{1,0:T(8,128)(2,1)}, u32[]{:S(2)}) copy-start(bf16[64,6656]{1,0:T(8,128)(2,1)} %get-tuple-element.5) | copy-start | bytes 2555908
